TPU v7x, 32 devices: a whole 2x2x4 slice. The times are simulated.
32 devices in a mesh: ang: 4 (over y, x), snap: 8 (over z, core).
Axes of the slice: x: 2, y: 2, z: 4, core: 2. Of those that a mesh axis runs over, the one named last changes fastest.
Arguments:
- cube: bfloat16 [2, 512, 8192], P(None, None, 'snap'), may hold values from -24 to 24
- select: int32 [1024], P('snap'), may hold values from 0 to 8191, as said below
- phases: int32 [16], replicated, may hold values from 0 to 63
- jitter: float32 [2, 512], replicated, may hold values from -0.4 to 0.4
Outputs:
- powers: float32 [16384], P(('ang', 'snap'))
Inputs may be any that keep to these rules, and one draw needn't show every extreme that they name: `select`: the selections of snapshot block j (entries j * 128 to (j + 1) * 128 - 1) lie in cell block j (cells j * 1024 to (j + 1) * 1024 - 1).
All inputs are finite; a program needn't handle non-finite values.
Results may differ from a plain program's by a relative error of at most 0.0012.
Values sent between devices are 32-bit elements; how exact they have to be, the bound alone decides.
No kernel may reach another device: no remote copies, remote signals or barrier semaphores. Data moves between devices by JAX's collectives and lax.ppermute only.
A program may use at most 128 MiB of HBM per device.

v0:
```python
import functools
import math

import jax
import jax.numpy as jnp
from jax import lax
from jax.experimental import pallas as pl
from jax.experimental.pallas import tpu as pltpu
from jax.sharding import PartitionSpec as P


RX = 32
GU = 128
GV = 128
Q = 64
ITERS = 3
K = GU * GV

TILE = 128
PAIR = 2 * TILE
WIDTH = 2048
PANEL = 16
AHEAD = 6
F32 = jnp.float32
BF16 = jnp.bfloat16


def nt_dot(left, right):
    return lax.dot_general(left, right, (((1,), (1,)), ((), ())), preferred_element_type=F32)


def dot(left, right):
    return jnp.dot(left, right, preferred_element_type=F32)


def split(x):
    high = x.astype(BF16)
    return high, (x - high.astype(F32)).astype(BF16)


def dot3(left, right):
    left_high, left_low = split(left)
    right_high, right_low = split(right)
    return dot(left_high, right_high) + (dot(left_low, right_high) + dot(left_high, right_low))


def take(x, index):
    return jnp.take_along_axis(x, index, axis=1, mode="promise_in_bounds")


def cost(microseconds):
    return pl.CostEstimate(flops=microseconds * 10**9, bytes_accessed=microseconds * 3 * 10**6, transcendentals=0)


def block_groups(blocks):
    groups = ([], [])
    for a in range(blocks):
        reach = blocks // 2 + (1 if a < blocks // 2 or blocks % 2 else 0)
        groups[a % 2].append((a, [(a + r) % blocks for r in range(reach)]))
    return groups


def group_pairs(group):
    return [(a, b) for a, partners in group for b in partners]


def complex_block(gram):
    real = gram[:TILE, :TILE] + gram[TILE:, TILE:]
    imag = gram[TILE:, :TILE] - gram[:TILE, TILE:]
    return real, imag


def steering_kernel(steps, *refs):
    start_real, start_imag, col_real, col_imag, turn_real, turn_imag, out_ref = refs
    spot = jnp.full((TILE, GV), pl.program_id(0), jnp.int32)

    def block(b, _):
        rows = pl.ds(pl.multiple_of(b * TILE, TILE), TILE)
        first_real, first_imag = take(start_real[rows, :], spot), take(start_imag[rows, :], spot)
        across_real, across_imag = col_real[rows, :], col_imag[rows, :]
        real = across_real * first_real - across_imag * first_imag
        imag = across_real * first_imag + across_imag * first_real
        by_real, by_imag = turn_real[rows, :], turn_imag[rows, :]
        for step in range(steps):
            if step:
                real, imag = real * by_real - imag * by_imag, real * by_imag + imag * by_real
            columns = slice(step * GV, (step + 1) * GV)
            out_ref[0, b, :TILE, columns] = real.astype(BF16)
            out_ref[0, b, TILE:, columns] = imag.astype(BF16)
        return 0

    lax.fori_loop(0, out_ref.shape[1], block, 0)


def all_steering(phases, jitter, width):
    channels = phases.shape[0] * RX
    blocks = channels // TILE
    steps = width // GV
    chunks = K // width
    channel = jnp.arange(channels, dtype=jnp.int32)
    position_x = (channel % RX).astype(F32) + jitter[0]
    position_y = (channel // RX).astype(F32) + jitter[1]
    offsets = jnp.broadcast_to(phases[:, None], (phases.shape[0], RX)).reshape(channels).astype(F32)
    lane = jnp.arange(GV, dtype=jnp.int32)
    row_angle = (2 * steps * lane - GU).astype(F32) / GU
    col_angle = (2 * lane - GV).astype(F32) / GV
    start = math.pi * (position_x[:, None] * row_angle[None, :])
    col = math.pi * (position_y[:, None] * col_angle[None, :]) + 2.0 * math.pi / Q * offsets[:, None]
    turn = jnp.broadcast_to((math.pi * 2.0 / GU) * position_x[:, None], (channels, GV))
    angles = jnp.stack([start, col, turn])
    real, imag = jnp.cos(angles), jnp.sin(angles)
    spec = pl.BlockSpec((channels, GV), lambda s: (0, 0))
    return pl.pallas_call(
        functools.partial(steering_kernel, steps),
        grid=(chunks,),
        in_specs=[spec] * 6,
        out_specs=pl.BlockSpec((1, blocks, PAIR, width), lambda s: (s, 0, 0, 0)),
        out_shape=jax.ShapeDtypeStruct((chunks, blocks, PAIR, width), BF16),
        name="steering",
        cost_estimate=cost(17),
    )(real[0], imag[0], real[1], imag[1], real[2], imag[2])


def own_block(shape, owned):
    per = shape[3] // owned
    return pl.BlockSpec((1, shape[1], PAIR, owned), lambda s, m: (m[0] // per, 0, 0, m[0] % per))


def sample_kernel(pairs, cube_ref, select_ref, column_ref, gram_ref, shots_ref):
    cells = cube_ref.shape[2]
    shots = select_ref.shape[1]
    chosen = lax.broadcasted_iota(jnp.int32, (cells, shots), 0) == select_ref[...]
    chosen = jnp.where(chosen, 1.0, 0.0).astype(BF16)
    across = lax.broadcasted_iota(jnp.int32, (shots, cells), 1) == column_ref[...]
    across = jnp.where(across, 1.0, 0.0).astype(BF16)
    blocks = cube_ref.shape[1] // TILE
    picked = []
    for block in range(blocks):
        rows = slice(block * TILE, (block + 1) * TILE)
        both = jnp.concatenate([cube_ref[0, rows, :], cube_ref[1, rows, :]], axis=0)
        picked.append(dot(both, chosen).astype(BF16))
        flat = nt_dot(across, both)
        columns = slice(block * PAIR, (block + 1) * PAIR)
        shots_ref[:shots, columns] = flat.astype(BF16)
        shots_ref[shots:, columns] = jnp.concatenate([flat[:, TILE:], -flat[:, :TILE]], axis=1).astype(BF16)
    for index, (a, b) in enumerate(pairs):
        real, imag = complex_block(nt_dot(picked[a], picked[b]))
        gram_ref[2 * index] = real
        gram_ref[2 * index + 1] = imag


def sample_terms(cube, select, pairs):
    shots = select.shape[0]
    return pl.pallas_call(
        functools.partial(sample_kernel, pairs),
        out_shape=[
            jax.ShapeDtypeStruct((2 * len(pairs), TILE, TILE), F32),
            jax.ShapeDtypeStruct((2 * shots, 2 * cube.shape[1]), BF16),
        ],
        name="sample",
        cost_estimate=cost(4),
    )(cube, select[None, :], select[:, None])


def beam_kernel(where_ref, steering_ref, shots_ref, out_ref):
    vectors = steering_ref[0].reshape(shots_ref.shape[1], steering_ref.shape[3])
    beams = dot(shots_ref[...], vectors)
    out_ref[0] = jnp.sum(beams * beams, axis=0, keepdims=True)


def local_energy(where, steering, shots, owned):
    width = steering.shape[3]
    near = lax.axis_size("snap") * owned // width
    per = width // owned
    grid_spec = pltpu.PrefetchScalarGridSpec(
        num_scalar_prefetch=1,
        grid=(near,),
        in_specs=[
            pl.BlockSpec((1, *steering.shape[1:]), lambda s, m: (m[0] // (per * near) * near + s, 0, 0, 0)),
            pl.BlockSpec(shots.shape, lambda s, m: (0, 0)),
        ],
        out_specs=pl.BlockSpec((1, 1, width), lambda s, m: (s, 0, 0)),
    )
    return pl.pallas_call(
        beam_kernel,
        grid_spec=grid_spec,
        out_shape=jax.ShapeDtypeStruct((near, 1, width), F32),
        name="beams",
        cost_estimate=cost(5),
    )(where, steering, shots).reshape(near * per, owned)


def swap(x, axis, mask):
    size = lax.axis_size(axis)
    return lax.ppermute(x, axis, [(i, i ^ mask) for i in range(size)])


def halve(x, axis, bit):
    half = x.shape[0] // 2
    high = (lax.axis_index(axis) >> bit) % 2
    keep = lax.dynamic_slice_in_dim(x, high * half, half, 0)
    give = lax.dynamic_slice_in_dim(x, (1 - high) * half, half, 0)
    return keep + swap(give, axis, 1 << bit)


def piece_start(index, size, rows):
    start = 0
    for bit in range(size.bit_length() - 1):
        rows = rows // 2
        start = start + (index >> bit) % 2 * rows
    return start


def scatter_energy(rows):
    snap, index = lax.axis_size("snap"), lax.axis_index("snap")
    halves = rows.reshape(snap // 2, 2, rows.shape[1])
    core, high = index % 2, index // 2
    mine = lax.dynamic_index_in_dim(halves, core, 1, keepdims=False)
    give = lax.dynamic_index_in_dim(halves, 1 - core, 1, keepdims=False)
    both = mine + swap(give, "snap", 1)
    total = lax.dynamic_slice_in_dim(both, high, 1, 0)
    for m in range(1, snap // 2):
        total = total + swap(lax.dynamic_slice_in_dim(both, high ^ m, 1, 0), "snap", 2 * m)
    return total


def gather_relative(x):
    snap, ang = lax.axis_size("snap"), lax.axis_size("ang")
    x = jnp.concatenate([x, swap(x, "snap", 1)], axis=0)
    x = jnp.concatenate([x] + [swap(x, "snap", m) for m in range(2, snap, 2)], axis=0)
    return [x] + [swap(x, "ang", m) for m in range(1, ang)]


def covariance_kernel(slots, table_ref, steering_ref, *refs):
    *parts, out_ref, powers_ref, scaled, total = refs
    step = pl.program_id(0)
    owned = powers_ref.shape[1]
    per = steering_ref.shape[3] // owned
    low = table_ref[0] % per

    @pl.when(step == 0)
    def _():
        total[...] = jnp.zeros_like(total)
        for n, part in enumerate(parts):
            powers_ref[n * part.shape[0] : (n + 1) * part.shape[0], :] = part[...]

    weights = jnp.concatenate([powers_ref[pl.ds(step * per + (q ^ low), 1), :] for q in range(per)], axis=1)
    used = max(slots) + 1
    for slot in range(used):
        scaled[slot] = (steering_ref[0, table_ref[1 + slot]].astype(F32) * weights).astype(BF16)
    for n, slot in enumerate(slots):
        total[n] += nt_dot(scaled[slot], steering_ref[0, table_ref[1 + used + n]])

    @pl.when(step == pl.num_programs(0) - 1)
    def _():
        for n in range(len(slots)):
            real, imag = complex_block(total[n])
            out_ref[2 * n] = real
            out_ref[2 * n + 1] = imag


def covariance_half(table, steering, powers, slots):
    chunks, blocks, pair, width = steering.shape
    rows, owned = powers[0].shape
    per = width // owned
    count = len(slots)
    grid_spec = pltpu.PrefetchScalarGridSpec(
        num_scalar_prefetch=1,
        grid=(chunks,),
        in_specs=[
            pl.BlockSpec((1, blocks, pair, width), lambda s, t: (s ^ (t[0] // per), 0, 0, 0)),
        ]
        + [pl.BlockSpec((rows, owned), lambda s, t: (0, 0))] * len(powers),
        out_specs=pl.BlockSpec((2 * count, TILE, TILE), lambda s, t: (0, 0, 0)),
        scratch_shapes=[
            pltpu.VMEM((rows * len(powers), owned), F32),
            pltpu.VMEM((max(slots) + 1, PAIR, width), BF16),
            pltpu.VMEM((count, PAIR, PAIR), F32),
        ],
    )
    return pl.pallas_call(
        functools.partial(covariance_kernel, slots),
        grid_spec=grid_spec,
        out_shape=jax.ShapeDtypeStruct((2 * count, TILE, TILE), F32),
        name="covariance",
        cost_estimate=cost(17),
    )(table, steering, *powers)


def embed(store, i, j, real, imag):
    top, left = i * PAIR, j * PAIR
    store(slice(top, top + TILE), slice(left, left + TILE), real)
    store(slice(top, top + TILE), slice(left + TILE, left + PAIR), -imag)
    store(slice(top + TILE, top + PAIR), slice(left, left + TILE), imag)
    store(slice(top + TILE, top + PAIR), slice(left + TILE, left + PAIR), real)


def spread_kernel(pairs, size, where_ref, *refs):
    *parts, high_ref, low_ref, whole = refs
    half = size // 2
    piece = parts[0].shape[0] // half
    for core, part in enumerate(parts):
        for n in range(half):
            start = piece_start((where_ref[0] % size) ^ (2 * n + core), size, whole.shape[0])
            whole[pl.ds(pl.multiple_of(start, 8), piece), :] = part[n * piece : (n + 1) * piece, :]

    def store(rows, columns, value):
        high, low = split(value)
        high_ref[rows, columns] = high
        low_ref[rows, columns] = low

    for index, (a, b) in enumerate(pairs):
        real = whole[2 * index * TILE : (2 * index + 1) * TILE, :]
        imag = whole[(2 * index + 1) * TILE : (2 * index + 2) * TILE, :]
        embed(store, a, b, real, imag)
        if a != b:
            embed(store, b, a, real.T, -imag.T)


def spread(where, parts, pairs, order):
    size = lax.axis_size("snap")
    whole = lambda shape: pl.BlockSpec(shape, lambda s, m: (0, 0))
    return pl.pallas_call(
        functools.partial(spread_kernel, pairs, size),
        grid_spec=pltpu.PrefetchScalarGridSpec(
            num_scalar_prefetch=1,
            grid=(1,),
            in_specs=[whole(part.shape) for part in parts],
            out_specs=[whole((order, order))] * 2,
            scratch_shapes=[pltpu.VMEM((2 * len(pairs) * TILE, TILE), F32)],
        ),
        out_shape=[jax.ShapeDtypeStruct((order, order), BF16)] * 2,
        name="spread",
        cost_estimate=cost(3),
    )(where, *parts)


def invert_tile(tile):
    lane_all = lax.broadcasted_iota(jnp.int32, (TILE, TILE), 1)
    lane = lax.broadcasted_iota(jnp.int32, (PANEL, TILE), 1)
    sublane = lax.broadcasted_iota(jnp.int32, (PANEL, TILE), 0)

    def panel(step, _):
        base = pl.multiple_of(step * PANEL, PANEL)
        row_real, row_imag = tile[pl.ds(base, PANEL), :TILE], tile[pl.ds(base, PANEL), TILE:]

        def spread_column(j):
            spot = jnp.full((PANEL, TILE), base + j, jnp.int32)
            return take(row_real, spot), take(row_imag, spot)

        columns = {j: spread_column(j) for j in range(AHEAD)}
        real, imag = tile[:, :TILE], tile[:, TILE:]
        pattern = base + lane_all % PANEL
        sides = jnp.where((lane_all // PANEL) % 2 == 0, take(real, pattern), take(imag, pattern))
        high = sides.astype(BF16).astype(F32)
        left = jnp.where(lane_all // (2 * PANEL) == 1, sides - high, high).astype(BF16)
        for p in range(PANEL):
            if p + AHEAD < PANEL:
                columns[p + AHEAD] = spread_column(p + AHEAD)
            here = sublane == p
            hit = lane == base + p
            own_real, own_imag = columns.pop(p)
            inverse = 1.0 / own_real[p : p + 1, :]
            own_real = jnp.where(here, 1.0 - inverse, own_real * inverse)
            own_imag = jnp.where(here, 0.0, own_imag * inverse)

            def reduce(real, imag):
                pivot_real, pivot_imag = real[p : p + 1, :], imag[p : p + 1, :]
                return (
                    real - (own_real * pivot_real - own_imag * pivot_imag),
                    imag - (own_real * pivot_imag + own_imag * pivot_real),
                )

            row_real = jnp.where(hit, jnp.where(here, 1.0, 0.0), row_real)
            row_imag = jnp.where(hit, 0.0, row_imag)
            row_real, row_imag = reduce(row_real, row_imag)
            for j in columns:
                columns[j] = reduce(*columns[j])
        rows = jnp.concatenate([row_real, row_imag], axis=1)
        high, low = split(rows)
        turned_high = jnp.concatenate([-high[:, TILE:], high[:, :TILE]], axis=1)
        turned_low = jnp.concatenate([-low[:, TILE:], low[:, :TILE]], axis=1)
        right = [high, turned_high, high, turned_high, low, turned_low]
        right += [jnp.zeros_like(low)] * (TILE // PANEL - len(right))
        update = dot(left, jnp.concatenate(right, axis=0))
        inside = lane_all // PANEL == step
        tile[:, :TILE] = jnp.where(inside, 0.0, real) - update[:, :TILE]
        tile[:, TILE:] = jnp.where(inside, 0.0, imag) - update[:, TILE:]
        tile[pl.ds(base, PANEL), :] = rows
        return 0

    lax.fori_loop(0, TILE // PANEL, panel, 0)


def step_kernel(
    pairs, shots, where_ref, mine_ref, other_ref, steering_ref, high_ref, low_ref, out_ref, matrix, tile, inv_high, inv_low
):
    order = matrix.shape[0]
    blocks = order // TILE

    def rows(i):
        return slice(i * TILE, (i + 1) * TILE)

    def cols(i, part):
        return slice(part * order + i * TILE, part * order + (i + 1) * TILE)

    def put(group, ref):
        for index, (a, b) in enumerate(pairs[group]):
            real, imag = ref[2 * index], ref[2 * index + 1]
            if a == b:
                matrix[rows(a), cols(a, 0)] = 0.5 * (real + real.T)
                matrix[rows(a), cols(a, 1)] = 0.5 * (imag - imag.T)
            else:
                matrix[rows(a), cols(b, 0)] = real
                matrix[rows(a), cols(b, 1)] = imag
                matrix[rows(b), cols(a, 0)] = real.T
                matrix[rows(b), cols(a, 1)] = -imag.T

    @pl.when(where_ref[1] == 0)
    def _():
        put(0, mine_ref)
        put(1, other_ref)

    @pl.when(where_ref[1] != 0)
    def _():
        put(1, mine_ref)
        put(0, other_ref)

    diagonal = lax.broadcasted_iota(jnp.int32, (TILE, TILE), 0) == lax.broadcasted_iota(jnp.int32, (TILE, TILE), 1)
    trace = jnp.zeros((1, 1), F32)
    for i in range(blocks):
        kept = jnp.where(diagonal, matrix[rows(i), cols(i, 0)], 0.0)
        trace = trace + jnp.sum(jnp.sum(kept, axis=0, keepdims=True), axis=1, keepdims=True)
    matrix[...] = matrix[...] * (1.0 / trace)
    for i in range(blocks):
        matrix[rows(i), cols(i, 0)] += jnp.where(diagonal, 1.0 / order, 0.0)

    unit = jnp.where(diagonal, 1.0, 0.0)
    nothing = jnp.zeros((TILE, TILE), F32)
    for k in range(blocks):
        tile[:, :TILE] = matrix[rows(k), cols(k, 0)]
        tile[:, TILE:] = matrix[rows(k), cols(k, 1)]
        invert_tile(tile)
        column = jnp.concatenate([matrix[:, cols(k, 0)], matrix[:, cols(k, 1)]], axis=1)
        matrix[rows(k), cols(k, 0)] = unit
        matrix[rows(k), cols(k, 1)] = nothing
        row_real, row_imag = matrix[rows(k), :order], matrix[rows(k), order:]
        panel = jnp.concatenate([row_real, row_imag], axis=1)
        turned = jnp.concatenate([-row_imag, row_real], axis=1)
        row = dot3(tile[...], jnp.concatenate([panel, turned], axis=0))
        row_turned = jnp.concatenate([-row[:, order:], row[:, :order]], axis=1)
        tall = jnp.concatenate([row, row_turned], axis=0)
        for i in range(blocks):
            if i == k:
                matrix[rows(k), :] = row
            else:
                matrix[rows(i), cols(k, 0)] = nothing
                matrix[rows(i), cols(k, 1)] = nothing
                matrix[rows(i), :] -= dot3(column[rows(i)], tall)

    def store(at_rows, at_columns, value):
        high, low = split(value)
        inv_high[at_rows, at_columns] = high
        inv_low[at_rows, at_columns] = low

    weights = []
    for i in range(blocks):
        for j in range(blocks):
            real, imag = matrix[rows(i), cols(j, 0)], matrix[rows(i), cols(j, 1)]
            if i == j:
                weight = jnp.sum(jnp.where(diagonal, real, 0.0), axis=1, keepdims=True)
                weights += [weight, weight]
                real = jnp.where(diagonal, 0.0, real)
            embed(store, i, j, real, imag)
    vectors = steering_ref[0].reshape(2 * order, steering_ref.shape[3])
    wide = vectors.astype(F32)
    solved = dot(inv_high[...], vectors) + dot(inv_low[...], vectors) + jnp.concatenate(weights, axis=0) * wide
    norms = jnp.sum(solved * wide, axis=0, keepdims=True)
    near = solved.astype(BF16)
    turned = dot(high_ref[...], near) + dot(low_ref[...], near)
    energy = jnp.sum(turned * solved, axis=0, keepdims=True)
    out_ref[...] = energy / (shots * norms * norms)


def next_powers(where, mine, other, steering, sample, owned, pairs, shots):
    blocks = steering.shape[1]
    order = blocks * TILE
    whole = lambda *shape: pl.BlockSpec(shape, lambda s, m: (0,) * len(shape))
    grid_spec = pltpu.PrefetchScalarGridSpec(
        num_scalar_prefetch=1,
        grid=(1,),
        in_specs=[
            whole(*mine.shape),
            whole(*other.shape),
            own_block(steering.shape, owned),
            whole(2 * order, 2 * order),
            whole(2 * order, 2 * order),
        ],
        out_specs=whole(1, owned),
        scratch_shapes=[
            pltpu.VMEM((order, 2 * order), F32),
            pltpu.VMEM((TILE, PAIR), F32),
            pltpu.VMEM((2 * order, 2 * order), BF16),
            pltpu.VMEM((2 * order, 2 * order), BF16),
        ],
    )
    return pl.pallas_call(
        functools.partial(step_kernel, pairs, shots),
        grid_spec=grid_spec,
        out_shape=jax.ShapeDtypeStruct((1, owned), F32),
        name="step",
        cost_estimate=cost(35),
        compiler_params=pltpu.CompilerParams(vmem_limit_bytes=56 * 1024 * 1024),
    )(where, mine, other, steering, *sample)


def shards(cube, select, phases, jitter):
    snap_count, ang_count = lax.axis_size("snap"), lax.axis_size("ang")
    snap_index, ang_index = lax.axis_index("snap"), lax.axis_index("ang")
    channels = cube.shape[1]
    shots = select.shape[0] * snap_count
    owned = K // (ang_count * snap_count)
    groups = block_groups(channels // TILE)
    pairs = [group_pairs(group) for group in groups]
    slots = [slot for slot, (a, partners) in enumerate(groups[0]) for b in partners]
    core = snap_index % 2
    me = (ang_index * snap_count + snap_index).astype(jnp.int32)
    where = jnp.stack([me, core.astype(jnp.int32)])
    flat = [
        jnp.array([a for a, partners in group] + [b for a, b in group_pairs(group)], jnp.int32) for group in groups
    ]
    table = jnp.concatenate([me[None], jnp.where(core == 0, flat[0], flat[1])])

    steering = all_steering(phases, jitter, max(owned, WIDTH))
    every = [(a, b) for a in range(channels // TILE) for b in range(a + 1)]
    gram, rows = sample_terms(cube, select - snap_index * cube.shape[2], every)
    piece = halve(halve(gram.reshape(-1, TILE), "snap", 0), "snap", 1)
    steering, piece = lax.optimization_barrier((steering, piece))
    energy = local_energy(where, steering, rows, owned)
    powers = scatter_energy(energy) / float(shots * channels * channels)
    for bit in range(2, snap_count.bit_length() - 1):
        piece = halve(piece, "snap", bit)

    def iteration(gathered):
        mine = covariance_half(table, steering, gathered, slots)
        other = swap(mine, "snap", 1)
        return next_powers(where, mine, other, steering, sample, owned, pairs, float(shots))

    gathered = gather_relative(powers)
    gathered, piece = lax.optimization_barrier((gathered, piece))

    others = []
    for m in range(2, snap_count, 2):
        others.append(swap(piece, "snap", m))
    both = jnp.concatenate([piece] + others, axis=0)
    parts = [both, swap(both, "snap", 1)]
    sample = spread(where, parts, every, 2 * channels)
    powers = iteration(gathered)
    return lax.fori_loop(1, ITERS, lambda _, powers: iteration(gather_relative(powers)), powers)[0]


def solution(mesh):
    return jax.shard_map(
        shards,
        mesh=mesh,
        in_specs=(P(None, None, "snap"), P("snap"), P(), P()),
        out_specs=P(("ang", "snap")),
        check_vma=False,
    )
```

profile of v0, /device:TPU:0, one launch (start us, length us, event | category | flops | bytes accessed | tf_op | source)
XLA Modules:
  0.0 275.2 jit_solution(2414700794518441903)
XLA Ops:
  2.0 4.4 %sample.1 = (f32[20,128,128]{2,1,0:T(8,128)}, bf16[256,1024]{1,0:T(8,128)(2,1)}) custom-call(bf16[2,512,1024]{2,1,0:T(8,128)(2,1)} %cube_ref.1, s32[1,128]{1,0:T(1,128)} %get-tuple-element.96.select_ref, s32[128,1]{1,0:T(8,128)} %copy.7.column_ref), custom_call_target="tpu_custom_call" | custom-call | flops 4000000000 | bytes 12000000 | tf_op jit(solution)/shard_map/sample/pallas_call | solution.py:154
  8.8 2.8 %fusion = (f32[3,512,128]{2,1,0:T(8,128)S(1)}, f32[3,512,128]{2,1,0:T(8,128)S(1)}) fusion(f32[1,512,128]{2,1,0:T(8,128)S(1)} %stack_broadcast_in_dim.8, f32[1,512,128]{2,1,0:T(8,128)S(1)} %multiply_add_fusion, f32[1,512,128]{2,1,0:T(8,128)S(1)} %multiply_multiply_fusion), kind=kLoop, calls=%fused_computation.2 | loop fusion | flops 393216 | bytes 2359296 | tf_op jit(solution)/shard_map/sin | solution.py:111
  13.5 2.6 collective-permute-start.9
  16.2 17.1 %steering.1.steering_ref = bf16[8,4,256,2048]{3,2,1,0:T(8,128)(2,1)} custom-call(f32[512,128]{1,0:T(8,128)} %get-tuple-element.84.refs_0_, f32[512,128]{1,0:T(8,128)} %get-tuple-element.81.refs_1_, f32[512,128]{1,0:T(8,128)} %get-tuple-element.83.refs_2_, f32[512,128]{1,0:T(8,128)} %get-tuple-element.80.refs_3_, f32[512,128]{1,0:T(8,128)} %get-tuple-element.82.refs_4_, ...), custom_call_target="tpu_custom_call" | custom-call | flops 16999999488 | bytes 51000000 | tf_op jit(solution)/shard_map/steering/pallas_call | solution.py:113
  33.4 6.1 %beams.1 = f32[2,1,2048]{2,1,0:T(1,128)} custom-call(s32[2]{0:T(128)S(1)} %pad_add_fusion.where_ref, bf16[8,4,256,2048]{3,2,1,0:T(8,128)(2,1)} %steering.1.steering_ref, bf16[256,1024]{1,0:T(8,128)(2,1)} %get-tuple-element.55.shots_ref), custom_call_target="tpu_custom_call" | custom-call | flops 5000000000 | bytes 15000000 | tf_op jit(solution)/shard_map/beams/pallas_call | solution.py:184
  41.8 2.9 %collective-permute-start.12 = (f32[1,512]{1,0:T(1,128)S(1)}, f32[1,512]{1,0:T(1,128)S(1)}, u32[]{:S(2)}, u32[]{:S(2)}) collective-permute-start(f32[1,512]{1,0:T(1,128)S(1)} %get-tuple-element.91), channel_id=1, source_target_pairs={{0,4},{1,5},{2,6},{3,7},{4,0},{5,1},{6,2},{7,3},{8,12},{9,13},{10,... | collective-permute-start | bytes 6152 | tf_op jit(solution)/shard_map/ppermute | solution.py:195
  46.3 3.8 %collective-permute-done.13 = f32[1,512]{1,0:T(1,128)S(1)} collective-permute-done((f32[1,512]{1,0:T(1,128)S(1)}, f32[1,512]{1,0:T(1,128)S(1)}, u32[]{:S(2)}, u32[]{:S(2)}) %collective-permute-start.13) | collective-permute-done | bytes 2080 | tf_op jit(solution)/shard_map/ppermute | solution.py:195
  53.3 2.4 collective-permute-start.17
  55.7 5.0 %collective-permute-done.16 = f32[2,512]{1,0:T(2,128)S(1)} collective-permute-done((f32[2,512]{1,0:T(2,128)S(1)}, f32[2,512]{1,0:T(2,128)S(1)}, u32[]{:S(2)}, u32[]{:S(2)}) %collective-permute-start.16) | collective-permute-done | bytes 4128 | tf_op jit(solution)/shard_map/ppermute | solution.py:195
  66.1 2.4 collective-permute-done.20.refs_3_
  69.2 1.9 collective-permute-start.24
  71.1 1.9 collective-permute-start.25
  73.0 3.4 %collective-permute-done.23 = f32[320,128]{1,0:T(8,128)S(1)} collective-permute-done((f32[320,128]{1,0:T(8,128)S(1)}, f32[320,128]{1,0:T(8,128)S(1)}, u32[]{:S(2)}, u32[]{:S(2)}) %collective-permute-start.23) | collective-permute-done | bytes 163872 | tf_op jit(solution)/shard_map/ppermute | solution.py:195
  76.5 6.2 %collective-permute-done.24 = f32[320,128]{1,0:T(8,128)S(1)} collective-permute-done((f32[320,128]{1,0:T(8,128)S(1)}, f32[320,128]{1,0:T(8,128)S(1)}, u32[]{:S(2)}, u32[]{:S(2)}) %collective-permute-start.24) | collective-permute-done | bytes 163872 | tf_op jit(solution)/shard_map/ppermute | solution.py:195
  82.8 18.6 %covariance.2.mine_ref = f32[10,128,128]{2,1,0:T(8,128)} custom-call(s32[8]{0:T(128)S(1)} %pad_add_fusion.1.table_ref, bf16[8,4,256,2048]{3,2,1,0:T(8,128)(2,1)} %steering.1.steering_ref, f32[8,512]{1,0:T(8,128)} %copy-done.4, f32[8,512]{1,0:T(8,128)} %copy-done.11, f32[8,512]{1,0:T(8,128)} %copy-done.12, f32[8,512]{1,0:T(8,128)} %copy-done.13), custom_call_target="tpu_custom_call" | custom-call | flops 16999999488 | bytes 51000000 | tf_op jit(solution)/shard_map/covariance/pallas_call | solution.py:281
  102.8 4.6 %spread.1 = (bf16[1024,1024]{1,0:T(8,128)(2,1)}, bf16[1024,1024]{1,0:T(8,128)(2,1)}) custom-call(s32[2]{0:T(128)S(1)} %pad_add_fusion.where_ref, f32[1280,128]{1,0:T(8,128)} %copy-done.3, f32[1280,128]{1,0:T(8,128)} %copy-done.8), custom_call_target="tpu_custom_call" | custom-call | flops 3000000000 | bytes 9000000 | tf_op jit(solution)/shard_map/spread/pallas_call | solution.py:323
  108.2 30.3 %step.2 = f32[1,512]{1,0:T(1,128)S(1)} custom-call(s32[2]{0:T(128)S(1)} %pad_add_fusion.where_ref, f32[10,128,128]{2,1,0:T(8,128)} %covariance.2.mine_ref, f32[10,128,128]{2,1,0:T(8,128)} %copy-done.9, bf16[8,4,256,2048]{3,2,1,0:T(8,128)(2,1)} %steering.1.steering_ref, bf16[1024,1024]{1,0:T(8,128)(2,1)} %get-tuple-element.147.high_ref, ...), custom_call_target="tpu_custom_call" | custom-call | flops 35000000512 | bytes 105000000 | tf_op jit(solution)/shard_map/step/pallas_call | solution.py:507
  138.5 136.1 %while.10 = (s32[]{:T(128)}, f32[1,512]{1,0:T(1,128)S(1)}, s32[8]{0:T(128)S(1)}, bf16[8,4,256,2048]{3,2,1,0:T(8,128)(2,1)}, s32[2]{0:T(128)S(1)}, /*index=5*/bf1...) while((s32[]{:T(128)}, f32[1,512]{1,0:T(1,128)S(1)}, s32[8]{0:T(128)S(1)}, ...), condition=%wide.region_1.2_spmd, body=%wide.region_0.1_spmd.sunk | while | flops 52000002048 | bytes 161800496 | solution.py:559
  140.0 2.5 collective-permute-start.1
  143.1 1.9 collective-permute-start.3
  144.9 2.1 collective-permute-done.2
  149.6 2.5 collective-permute-start.6
  154.9 18.6 %covariance.3.mine_ref = f32[10,128,128]{2,1,0:T(8,128)} custom-call(s32[8]{0:T(128)S(1)} %get-tuple-element.160.table_ref, bf16[8,4,256,2048]{3,2,1,0:T(8,128)(2,1)} %get-tuple-element.161.steering_ref, f32[8,512]{1,0:T(8,128)} %copy-done.1, f32[8,512]{1,0:T(8,128)} %copy-done.14, f32[8,512]{1,0:T(8,128)} %copy-done.15, f32[8,512]{1,0:T(8,128)} %copy-done.16), custom_call_target="tpu_custom_call" | custom-call | flops 16999999488 | bytes 51000000 | tf_op jit(solution)/shard_map/while/body/eval_jaxpr/covariance/pallas_call | solution.py:281
  173.4 2.3 collective-permute-done.7.other_ref
  176.6 29.4 %step.3 = f32[1,512]{1,0:T(1,128)S(1)} custom-call(s32[2]{0:T(128)S(1)} %get-tuple-element.162.where_ref, f32[10,128,128]{2,1,0:T(8,128)} %covariance.3.mine_ref, f32[10,128,128]{2,1,0:T(8,128)} %copy-done.10, bf16[8,4,256,2048]{3,2,1,0:T(8,128)(2,1)} %get-tuple-element.161.steering_ref, bf16[1024,1024]{1,0:T(8,128)(2,1)S(1)} %get-tuple-element.163.high_ref, ...), custom_call_target="tpu_custom_call" | custom-call | flops 35000000512 | bytes 105000000 | tf_op jit(solution)/shard_map/while/body/eval_jaxpr/step/pallas_call | solution.py:507
  207.5 2.3 collective-permute-start.2
  209.7 2.0 collective-permute-start.3
  212.0 3.2 %collective-permute-done.3 = f32[2,512]{1,0:T(2,128)S(1)} collective-permute-done((f32[2,512]{1,0:T(2,128)S(1)}, f32[2,512]{1,0:T(2,128)S(1)}, u32[]{:S(2)}, u32[]{:S(2)}) %collective-permute-start.3) | collective-permute-done | bytes 4128 | tf_op jit(solution)/shard_map/while/body/eval_jaxpr/ppermute | solution.py:195
  220.5 2.4 collective-permute-done.6.refs_3_
  223.5 18.6 %covariance.3.mine_ref = f32[10,128,128]{2,1,0:T(8,128)} custom-call(s32[8]{0:T(128)S(1)} %get-tuple-element.160.table_ref, bf16[8,4,256,2048]{3,2,1,0:T(8,128)(2,1)} %get-tuple-element.161.steering_ref, f32[8,512]{1,0:T(8,128)} %copy-done.1, f32[8,512]{1,0:T(8,128)} %copy-done.14, f32[8,512]{1,0:T(8,128)} %copy-done.15, f32[8,512]{1,0:T(8,128)} %copy-done.16), custom_call_target="tpu_custom_call" | custom-call | flops 16999999488 | bytes 51000000 | tf_op jit(solution)/shard_map/while/body/eval_jaxpr/covariance/pallas_call | solution.py:281
  242.1 2.3 collective-permute-done.7.other_ref
  245.2 29.4 %step.3 = f32[1,512]{1,0:T(1,128)S(1)} custom-call(s32[2]{0:T(128)S(1)} %get-tuple-element.162.where_ref, f32[10,128,128]{2,1,0:T(8,128)} %covariance.3.mine_ref, f32[10,128,128]{2,1,0:T(8,128)} %copy-done.10, bf16[8,4,256,2048]{3,2,1,0:T(8,128)(2,1)} %get-tuple-element.161.steering_ref, bf16[1024,1024]{1,0:T(8,128)(2,1)S(1)} %get-tuple-element.163.high_ref, ...), custom_call_target="tpu_custom_call" | custom-call | flops 35000000512 | bytes 105000000 | tf_op jit(solution)/shard_map/while/body/eval_jaxpr/step/pallas_call | solution.py:507
  (138 shorter events, 39.1 us)
Async XLA Ops:
  7.5 5.9 %collective-permute-start.8 = (f32[1280,128]{1,0:T(8,128)S(1)}, f32[1280,128]{1,0:T(8,128)S(1)}, u32[]{:S(2)}, u32[]{:S(2)}) collective-permute-start(f32[1280,128]{1,0:T(8,128)S(1)} %constant_dynamic-slice_fusion.8), channel_id=1, source_target_pairs={{0,1},{1,0},{2,3},{3,2},{4,5},{5,4},{6,7},{7,6},{8,9},{9,8},{10,11... | collective-permute-start | bytes 1966088 | tf_op jit(solution)/shard_map/ppermute | solution.py:195
  13.5 19.8 %collective-permute-start.9 = (f32[640,128]{1,0:T(8,128)S(1)}, f32[640,128]{1,0:T(8,128)S(1)}, u32[]{:S(2)}, u32[]{:S(2)}) collective-permute-start(f32[640,128]{1,0:T(8,128)S(1)} %constant_dynamic-slice_fusion.7), channel_id=1, source_target_pairs={{0,2},{1,3},{2,0},{3,1},{4,6},{5,7},{6,4},{7,5},{8,10},{9,11},{10,... | collective-permute-start | bytes 983048 | tf_op jit(solution)/shard_map/ppermute | solution.py:195
  40.3 1.2 collective-permute-start.10
  41.5 4.5 %collective-permute-start.11 = (f32[1,512]{1,0:T(1,128)S(1)}, f32[1,512]{1,0:T(1,128)S(1)}, u32[]{:S(2)}, u32[]{:S(2)}) collective-permute-start(f32[1,512]{1,0:T(1,128)S(1)} %get-tuple-element.89), channel_id=1, source_target_pairs={{0,2},{1,3},{2,0},{3,1},{4,6},{5,7},{6,4},{7,5},{8,10},{9,11},{10,... | collective-permute-start | bytes 6152 | tf_op jit(solution)/shard_map/ppermute | solution.py:195
  41.8 4.5 %collective-permute-start.12 = (f32[1,512]{1,0:T(1,128)S(1)}, f32[1,512]{1,0:T(1,128)S(1)}, u32[]{:S(2)}, u32[]{:S(2)}) collective-permute-start(f32[1,512]{1,0:T(1,128)S(1)} %get-tuple-element.91), channel_id=1, source_target_pairs={{0,4},{1,5},{2,6},{3,7},{4,0},{5,1},{6,2},{7,3},{8,12},{9,13},{10,... | collective-permute-start | bytes 6152 | tf_op jit(solution)/shard_map/ppermute | solution.py:195
  44.6 5.4 %collective-permute-start.13 = (f32[1,512]{1,0:T(1,128)S(1)}, f32[1,512]{1,0:T(1,128)S(1)}, u32[]{:S(2)}, u32[]{:S(2)}) collective-permute-start(f32[1,512]{1,0:T(1,128)S(1)} %get-tuple-element.90), channel_id=1, source_target_pairs={{0,6},{1,7},{2,4},{3,5},{4,2},{5,3},{6,0},{7,1},{8,14},{9,15},{10,... | collective-permute-start | bytes 6152 | tf_op jit(solution)/shard_map/ppermute | solution.py:195
  50.1 14.2 %collective-permute-start.21 = (f32[320,128]{1,0:T(8,128)S(1)}, f32[320,128]{1,0:T(8,128)S(1)}, u32[]{:S(2)}, u32[]{:S(2)}) collective-permute-start(f32[320,128]{1,0:T(8,128)S(1)} %constant_dynamic-slice_fusion), channel_id=1, source_target_pairs={{0,4},{1,5},{2,6},{3,7},{4,0},{5,1},{6,2},{7,3},{8,12},{9,13},{10,... | collective-permute-start | bytes 491528 | tf_op jit(solution)/shard_map/ppermute | solution.py:195
  51.3 4.5 %collective-permute-start.15 = (f32[2,512]{1,0:T(2,128)S(1)}, f32[2,512]{1,0:T(2,128)S(1)}, u32[]{:S(2)}, u32[]{:S(2)}) collective-permute-start(f32[2,512]{1,0:T(2,128)S(1)} %pad_maximum_fusion.2), channel_id=1, source_target_pairs={{0,2},{1,3},{2,0},{3,1},{4,6},{5,7},{6,4},{7,5},{8,10},{9,11},{10,... | collective-permute-start | bytes 12296 | tf_op jit(solution)/shard_map/ppermute | solution.py:195
  52.2 8.5 %collective-permute-start.16 = (f32[2,512]{1,0:T(2,128)S(1)}, f32[2,512]{1,0:T(2,128)S(1)}, u32[]{:S(2)}, u32[]{:S(2)}) collective-permute-start(f32[2,512]{1,0:T(2,128)S(1)} %pad_maximum_fusion.2), channel_id=1, source_target_pairs={{0,4},{1,5},{2,6},{3,7},{4,0},{5,1},{6,2},{7,3},{8,12},{9,13},{10,... | collective-permute-start | bytes 12296 | tf_op jit(solution)/shard_map/ppermute | solution.py:195
  53.3 7.4 %collective-permute-start.17 = (f32[2,512]{1,0:T(2,128)S(1)}, f32[2,512]{1,0:T(2,128)S(1)}, u32[]{:S(2)}, u32[]{:S(2)}) collective-permute-start(f32[2,512]{1,0:T(2,128)S(1)} %pad_maximum_fusion.2), channel_id=1, source_target_pairs={{0,6},{1,7},{2,4},{3,5},{4,2},{5,3},{6,0},{7,1},{8,14},{9,15},{10,... | collective-permute-start | bytes 12296 | tf_op jit(solution)/shard_map/ppermute | solution.py:195
  60.8 3.8 %collective-permute-start.18 = (f32[8,512]{1,0:T(8,128)S(1)}, f32[8,512]{1,0:T(8,128)S(1)}, u32[]{:S(2)}, u32[]{:S(2)}) collective-permute-start(f32[8,512]{1,0:T(8,128)S(1)} %concatenate.22.refs_0_), channel_id=1, source_target_pairs={{0,8},{8,0},{16,24},{24,16},{1,9},{9,1},{17,25},{25,17},{2,10},{10... | collective-permute-start | bytes 49160 | tf_op jit(solution)/shard_map/ppermute | solution.py:195
  62.3 3.7 %collective-permute-start.19 = (f32[8,512]{1,0:T(8,128)S(1)}, f32[8,512]{1,0:T(8,128)S(1)}, u32[]{:S(2)}, u32[]{:S(2)}) collective-permute-start(f32[8,512]{1,0:T(8,128)S(1)} %concatenate.22.refs_0_), channel_id=1, source_target_pairs={{0,16},{8,24},{16,0},{24,8},{1,17},{9,25},{17,1},{25,9},{2,18},{10... | collective-permute-start | bytes 49160 | tf_op jit(solution)/shard_map/ppermute | solution.py:195
  63.8 4.6 %collective-permute-start.20 = (f32[8,512]{1,0:T(8,128)S(1)}, f32[8,512]{1,0:T(8,128)S(1)}, u32[]{:S(2)}, u32[]{:S(2)}) collective-permute-start(f32[8,512]{1,0:T(8,128)S(1)} %concatenate.22.refs_0_), channel_id=1, source_target_pairs={{0,24},{8,16},{16,8},{24,0},{1,25},{9,17},{17,9},{25,1},{2,26},{10... | collective-permute-start | bytes 49160 | tf_op jit(solution)/shard_map/ppermute | solution.py:195
  68.5 8.0 %collective-permute-start.23 = (f32[320,128]{1,0:T(8,128)S(1)}, f32[320,128]{1,0:T(8,128)S(1)}, u32[]{:S(2)}, u32[]{:S(2)}) collective-permute-start(f32[320,128]{1,0:T(8,128)S(1)} %dynamic-slice_add_fusion.2), channel_id=1, source_target_pairs={{0,2},{1,3},{2,0},{3,1},{4,6},{5,7},{6,4},{7,5},{8,10},{9,11},{10,... | collective-permute-start | bytes 491528 | tf_op jit(solution)/shard_map/ppermute | solution.py:195
  69.2 13.5 %collective-permute-start.24 = (f32[320,128]{1,0:T(8,128)S(1)}, f32[320,128]{1,0:T(8,128)S(1)}, u32[]{:S(2)}, u32[]{:S(2)}) collective-permute-start(f32[320,128]{1,0:T(8,128)S(1)} %dynamic-slice_add_fusion.2), channel_id=1, source_target_pairs={{0,4},{1,5},{2,6},{3,7},{4,0},{5,1},{6,2},{7,3},{8,12},{9,13},{10,... | collective-permute-start | bytes 491528 | tf_op jit(solution)/shard_map/ppermute | solution.py:195
  71.1 11.6 %collective-permute-start.25 = (f32[320,128]{1,0:T(8,128)S(1)}, f32[320,128]{1,0:T(8,128)S(1)}, u32[]{:S(2)}, u32[]{:S(2)}) collective-permute-start(f32[320,128]{1,0:T(8,128)S(1)} %dynamic-slice_add_fusion.2), channel_id=1, source_target_pairs={{0,6},{1,7},{2,4},{3,5},{4,2},{5,3},{6,0},{7,1},{8,14},{9,15},{10,... | collective-permute-start | bytes 491528 | tf_op jit(solution)/shard_map/ppermute | solution.py:195
  82.7 19.2 %collective-permute-start.26 = (f32[1280,128]{1,0:T(8,128)S(1)}, f32[1280,128]{1,0:T(8,128)S(1)}, u32[]{:S(2)}, u32[]{:S(2)}) collective-permute-start(f32[1280,128]{1,0:T(8,128)S(1)} %constant_dynamic-update-slice_fusion.refs_0_), channel_id=1, source_target_pairs={{0,1},{1,0},{2,3},{3,2},{4,5},{5,4},{6,7},{7,6},{8,9},{9,8},{10,11... | collective-permute-start | bytes 1966088 | tf_op jit(solution)/shard_map/ppermute | solution.py:195
  101.4 6.0 %collective-permute-start.22 = (f32[10,128,128]{2,1,0:T(8,128)}, f32[10,128,128]{2,1,0:T(8,128)S(1)}, u32[]{:S(2)}, u32[]{:S(2)}) collective-permute-start(f32[10,128,128]{2,1,0:T(8,128)} %covariance.2.mine_ref), channel_id=1, source_target_pairs={{0,1},{1,0},{2,3},{3,2},{4,5},{5,4},{6,7},{7,6},{8,9},{9,8},{10,11... | collective-permute-start | bytes 1966088 | tf_op jit(solution)/shard_map/ppermute | solution.py:195
  140.0 4.9 %collective-permute-start.1 = (f32[2,512]{1,0:T(2,128)S(1)}, f32[2,512]{1,0:T(2,128)S(1)}, u32[]{:S(2)}, u32[]{:S(2)}) collective-permute-start(f32[2,512]{1,0:T(2,128)S(1)} %pad_maximum_fusion.4), channel_id=1, source_target_pairs={{0,2},{1,3},{2,0},{3,1},{4,6},{5,7},{6,4},{7,5},{8,10},{9,11},{10,... | collective-permute-start | bytes 12296 | tf_op jit(solution)/shard_map/while/body/eval_jaxpr/ppermute | solution.py:195
  142.5 4.5 %collective-permute-start.2 = (f32[2,512]{1,0:T(2,128)S(1)}, f32[2,512]{1,0:T(2,128)S(1)}, u32[]{:S(2)}, u32[]{:S(2)}) collective-permute-start(f32[2,512]{1,0:T(2,128)S(1)} %pad_maximum_fusion.4), channel_id=1, source_target_pairs={{0,4},{1,5},{2,6},{3,7},{4,0},{5,1},{6,2},{7,3},{8,12},{9,13},{10,... | collective-permute-start | bytes 12296 | tf_op jit(solution)/shard_map/while/body/eval_jaxpr/ppermute | solution.py:195
  143.1 5.4 %collective-permute-start.3 = (f32[2,512]{1,0:T(2,128)S(1)}, f32[2,512]{1,0:T(2,128)S(1)}, u32[]{:S(2)}, u32[]{:S(2)}) collective-permute-start(f32[2,512]{1,0:T(2,128)S(1)} %pad_maximum_fusion.4), channel_id=1, source_target_pairs={{0,6},{1,7},{2,4},{3,5},{4,2},{5,3},{6,0},{7,1},{8,14},{9,15},{10,... | collective-permute-start | bytes 12296 | tf_op jit(solution)/shard_map/while/body/eval_jaxpr/ppermute | solution.py:195
  148.5 3.8 %collective-permute-start.4 = (f32[8,512]{1,0:T(8,128)S(1)}, f32[8,512]{1,0:T(8,128)S(1)}, u32[]{:S(2)}, u32[]{:S(2)}) collective-permute-start(f32[8,512]{1,0:T(8,128)S(1)} %concatenate.25.refs_0_), channel_id=1, source_target_pairs={{0,8},{8,0},{16,24},{24,16},{1,9},{9,1},{17,25},{25,17},{2,10},{10... | collective-permute-start | bytes 49160 | tf_op jit(solution)/shard_map/while/body/eval_jaxpr/ppermute | solution.py:195
  149.1 3.7 %collective-permute-start.5 = (f32[8,512]{1,0:T(8,128)S(1)}, f32[8,512]{1,0:T(8,128)S(1)}, u32[]{:S(2)}, u32[]{:S(2)}) collective-permute-start(f32[8,512]{1,0:T(8,128)S(1)} %concatenate.25.refs_0_), channel_id=1, source_target_pairs={{0,16},{8,24},{16,0},{24,8},{1,17},{9,25},{17,1},{25,9},{2,18},{10... | collective-permute-start | bytes 49160 | tf_op jit(solution)/shard_map/while/body/eval_jaxpr/ppermute | solution.py:195
  149.6 4.6 %collective-permute-start.6 = (f32[8,512]{1,0:T(8,128)S(1)}, f32[8,512]{1,0:T(8,128)S(1)}, u32[]{:S(2)}, u32[]{:S(2)}) collective-permute-start(f32[8,512]{1,0:T(8,128)S(1)} %concatenate.25.refs_0_), channel_id=1, source_target_pairs={{0,24},{8,16},{16,8},{24,0},{1,25},{9,17},{17,9},{25,1},{2,26},{10... | collective-permute-start | bytes 49160 | tf_op jit(solution)/shard_map/while/body/eval_jaxpr/ppermute | solution.py:195
  173.4 2.3 collective-permute-start.7
  207.2 4.5 %collective-permute-start.1 = (f32[2,512]{1,0:T(2,128)S(1)}, f32[2,512]{1,0:T(2,128)S(1)}, u32[]{:S(2)}, u32[]{:S(2)}) collective-permute-start(f32[2,512]{1,0:T(2,128)S(1)} %pad_maximum_fusion.4), channel_id=1, source_target_pairs={{0,2},{1,3},{2,0},{3,1},{4,6},{5,7},{6,4},{7,5},{8,10},{9,11},{10,... | collective-permute-start | bytes 12296 | tf_op jit(solution)/shard_map/while/body/eval_jaxpr/ppermute | solution.py:195
  207.5 4.5 %collective-permute-start.2 = (f32[2,512]{1,0:T(2,128)S(1)}, f32[2,512]{1,0:T(2,128)S(1)}, u32[]{:S(2)}, u32[]{:S(2)}) collective-permute-start(f32[2,512]{1,0:T(2,128)S(1)} %pad_maximum_fusion.4), channel_id=1, source_target_pairs={{0,4},{1,5},{2,6},{3,7},{4,0},{5,1},{6,2},{7,3},{8,12},{9,13},{10,... | collective-permute-start | bytes 12296 | tf_op jit(solution)/shard_map/while/body/eval_jaxpr/ppermute | solution.py:195
  209.7 5.4 %collective-permute-start.3 = (f32[2,512]{1,0:T(2,128)S(1)}, f32[2,512]{1,0:T(2,128)S(1)}, u32[]{:S(2)}, u32[]{:S(2)}) collective-permute-start(f32[2,512]{1,0:T(2,128)S(1)} %pad_maximum_fusion.4), channel_id=1, source_target_pairs={{0,6},{1,7},{2,4},{3,5},{4,2},{5,3},{6,0},{7,1},{8,14},{9,15},{10,... | collective-permute-start | bytes 12296 | tf_op jit(solution)/shard_map/while/body/eval_jaxpr/ppermute | solution.py:195
  215.2 3.9 %collective-permute-start.4 = (f32[8,512]{1,0:T(8,128)S(1)}, f32[8,512]{1,0:T(8,128)S(1)}, u32[]{:S(2)}, u32[]{:S(2)}) collective-permute-start(f32[8,512]{1,0:T(8,128)S(1)} %concatenate.25.refs_0_), channel_id=1, source_target_pairs={{0,8},{8,0},{16,24},{24,16},{1,9},{9,1},{17,25},{25,17},{2,10},{10... | collective-permute-start | bytes 49160 | tf_op jit(solution)/shard_map/while/body/eval_jaxpr/ppermute | solution.py:195
  216.7 3.7 %collective-permute-start.5 = (f32[8,512]{1,0:T(8,128)S(1)}, f32[8,512]{1,0:T(8,128)S(1)}, u32[]{:S(2)}, u32[]{:S(2)}) collective-permute-start(f32[8,512]{1,0:T(8,128)S(1)} %concatenate.25.refs_0_), channel_id=1, source_target_pairs={{0,16},{8,24},{16,0},{24,8},{1,17},{9,25},{17,1},{25,9},{2,18},{10... | collective-permute-start | bytes 49160 | tf_op jit(solution)/shard_map/while/body/eval_jaxpr/ppermute | solution.py:195
  218.2 4.6 %collective-permute-start.6 = (f32[8,512]{1,0:T(8,128)S(1)}, f32[8,512]{1,0:T(8,128)S(1)}, u32[]{:S(2)}, u32[]{:S(2)}) collective-permute-start(f32[8,512]{1,0:T(8,128)S(1)} %concatenate.25.refs_0_), channel_id=1, source_target_pairs={{0,24},{8,16},{16,8},{24,0},{1,25},{9,17},{17,9},{25,1},{2,26},{10... | collective-permute-start | bytes 49160 | tf_op jit(solution)/shard_map/while/body/eval_jaxpr/ppermute | solution.py:195
  242.1 2.3 collective-permute-start.7
  (27 other events, 211.2 us)
where the time goes:
time: 276 us; the launch traced here: 275 us
  Pallas kernels  177 us (64%)
  waiting for transfers between devices  44.8 us (16%)
  starting transfers between devices  37.9 us (14%)
  local copies, waits for them, and re-layouts  9.47 us (3%)
  other arithmetic  5.43 us (2%)
    pallas_call x3, Pallas kernels, next_powers(): pl.pallas_call(functools.partial(step_kernel, pairs, shots), grid_spec=gr...  89.1 us
    pallas_call x3, Pallas kernels, covariance_half(): pl.pallas_call(functools.partial(covariance_kernel, slots), grid_spec=gri...  55.7 us
    ppermute x35, waiting for transfers between devices, swap(): return lax.ppermute(x, axis, [(i, i ^ mask) for i in range(size)])  44.8 us
    ppermute x35, starting transfers between devices, swap(): return lax.ppermute(x, axis, [(i, i ^ mask) for i in range(size)])  37.9 us
    pallas_call x1, Pallas kernels, all_steering(): pl.pallas_call(functools.partial(steering_kernel, steps), grid=(chunks,),...  17.1 us
    pallas_call x1, Pallas kernels, local_energy(): pl.pallas_call(beam_kernel, grid_spec=grid_spec, out_shape=jax.ShapeDtype...  6.05 us
  transfers between devices with their start and end apart: 35, of which 24 were waited for; matrix products, arithmetic and copies ran while one was open for 2% of the time, Pallas kernels for 15%

commit v1 on v0

--- a/solution.py
+++ b/solution.py
@@ -70,33 +70,8 @@
     return real, imag
 
 
-def steering_kernel(steps, *refs):
-    start_real, start_imag, col_real, col_imag, turn_real, turn_imag, out_ref = refs
-    spot = jnp.full((TILE, GV), pl.program_id(0), jnp.int32)
-
-    def block(b, _):
-        rows = pl.ds(pl.multiple_of(b * TILE, TILE), TILE)
-        first_real, first_imag = take(start_real[rows, :], spot), take(start_imag[rows, :], spot)
-        across_real, across_imag = col_real[rows, :], col_imag[rows, :]
-        real = across_real * first_real - across_imag * first_imag
-        imag = across_real * first_imag + across_imag * first_real
-        by_real, by_imag = turn_real[rows, :], turn_imag[rows, :]
-        for step in range(steps):
-            if step:
-                real, imag = real * by_real - imag * by_imag, real * by_imag + imag * by_real
-            columns = slice(step * GV, (step + 1) * GV)
-            out_ref[0, b, :TILE, columns] = real.astype(BF16)
-            out_ref[0, b, TILE:, columns] = imag.astype(BF16)
-        return 0
-
-    lax.fori_loop(0, out_ref.shape[1], block, 0)
-
-
-def all_steering(phases, jitter, width):
+def angle_tables(phases, jitter, steps):
     channels = phases.shape[0] * RX
-    blocks = channels // TILE
-    steps = width // GV
-    chunks = K // width
     channel = jnp.arange(channels, dtype=jnp.int32)
     position_x = (channel % RX).astype(F32) + jitter[0]
     position_y = (channel // RX).astype(F32) + jitter[1]
@@ -108,38 +83,101 @@
     col = math.pi * (position_y[:, None] * col_angle[None, :]) + 2.0 * math.pi / Q * offsets[:, None]
     turn = jnp.broadcast_to((math.pi * 2.0 / GU) * position_x[:, None], (channels, GV))
     angles = jnp.stack([start, col, turn])
-    real, imag = jnp.cos(angles), jnp.sin(angles)
-    spec = pl.BlockSpec((channels, GV), lambda s: (0, 0))
+    return jnp.cos(angles), jnp.sin(angles)
+
+
+def fill_blocks(chunk, first, real_ref, imag_ref, out_ref):
+    steps = out_ref.shape[3] // GV
+    spot = jnp.full((TILE, GV), chunk, jnp.int32)
+
+    def block(b, _):
+        rows = pl.ds(pl.multiple_of((first + b) * TILE, TILE), TILE)
+        first_real, first_imag = take(real_ref[0, rows, :], spot), take(imag_ref[0, rows, :], spot)
+        across_real, across_imag = real_ref[1, rows, :], imag_ref[1, rows, :]
+        real = across_real * first_real - across_imag * first_imag
+        imag = across_real * first_imag + across_imag * first_real
+        by_real, by_imag = real_ref[2, rows, :], imag_ref[2, rows, :]
+        for step in range(steps):
+            if step:
+                real, imag = real * by_real - imag * by_imag, real * by_imag + imag * by_real
+            columns = slice(step * GV, (step + 1) * GV)
+            out_ref[0, b, :TILE, columns] = real.astype(BF16)
+            out_ref[0, b, TILE:, columns] = imag.astype(BF16)
+        return 0
+
+    lax.fori_loop(0, out_ref.shape[1], block, 0, unroll=True)
+
+
+def near_kernel(chunk_of, where_ref, real_ref, imag_ref, shots_ref, out_ref, energy_ref, beams):
+    step = pl.program_id(1)
+    count = out_ref.shape[1]
+    fill_blocks(chunk_of(pl.program_id(0), where_ref), step * count, real_ref, imag_ref, out_ref)
+
+    @pl.when(step == 0)
+    def _():
+        beams[...] = jnp.zeros_like(beams)
+
+    beams[...] += dot(shots_ref[...], out_ref[0].reshape(count * PAIR, out_ref.shape[3]))
+
+    @pl.when(step == pl.num_programs(1) - 1)
+    def _():
+        energy_ref[0] = jnp.sum(beams[...] * beams[...], axis=0, keepdims=True)
+
+
+def far_kernel(chunk_of, where_ref, real_ref, imag_ref, before_ref, out_ref):
+    count = out_ref.shape[1]
+    fill_blocks(chunk_of(pl.program_id(0), where_ref), pl.program_id(1) * count, real_ref, imag_ref, out_ref)
+
+
+def fill_steering(where, tables, blocks, owned, width, mask, shots=None, before=None):
+    near = lax.axis_size("snap") * owned // width
+    per = width // owned
+    count = 2 - blocks % 2
+
+    def chunk_of(step, m):
+        return (m[0] // (per * near) ^ mask) * near + step
+
+    in_specs = [pl.BlockSpec(table.shape, lambda s, b, m: (0, 0, 0)) for table in tables]
+    out_specs = [pl.BlockSpec((1, count, PAIR, width), lambda s, b, m: (chunk_of(s, m), b, 0, 0))]
+    out_shape = [jax.ShapeDtypeStruct((K // width, blocks, PAIR, width), BF16)]
+    if before is None:
+        kernel, last, aliases = near_kernel, shots, {}
+        in_specs.append(pl.BlockSpec((shots.shape[0], count * PAIR), lambda s, b, m: (0, b)))
+        out_specs.append(pl.BlockSpec((1, 1, width), lambda s, b, m: (s, 0, 0)))
+        out_shape.append(jax.ShapeDtypeStruct((near, 1, width), F32))
+        scratch = [pltpu.VMEM((shots.shape[0], width), F32)]
+    else:
+        kernel, last, aliases, scratch = far_kernel, before, {3: 0}, []
+        in_specs.append(pl.BlockSpec(memory_space=pl.ANY))
     return pl.pallas_call(
-        functools.partial(steering_kernel, steps),
-        grid=(chunks,),
-        in_specs=[spec] * 6,
-        out_specs=pl.BlockSpec((1, blocks, PAIR, width), lambda s: (s, 0, 0, 0)),
-        out_shape=jax.ShapeDtypeStruct((chunks, blocks, PAIR, width), BF16),
-        name="steering",
-        cost_estimate=cost(17),
-    )(real[0], imag[0], real[1], imag[1], real[2], imag[2])
-
-
-def own_block(shape, owned):
-    per = shape[3] // owned
-    return pl.BlockSpec((1, shape[1], PAIR, owned), lambda s, m: (m[0] // per, 0, 0, m[0] % per))
-
-
-def sample_kernel(pairs, cube_ref, select_ref, column_ref, gram_ref, shots_ref):
+        functools.partial(kernel, chunk_of),
+        grid_spec=pltpu.PrefetchScalarGridSpec(
+            num_scalar_prefetch=1,
+            grid=(near, blocks // count),
+            in_specs=in_specs,
+            out_specs=out_specs,
+            scratch_shapes=scratch,
+        ),
+        out_shape=out_shape,
+        input_output_aliases=aliases,
+        name="near_steering" if before is None else "far_steering",
+        cost_estimate=cost(8 if before is None else 5),
+    )(where, *tables, last)
+
+
+def sample_kernel(pairs, cube_ref, select_ref, gram_ref, shots_ref):
     cells = cube_ref.shape[2]
     shots = select_ref.shape[1]
     chosen = lax.broadcasted_iota(jnp.int32, (cells, shots), 0) == select_ref[...]
     chosen = jnp.where(chosen, 1.0, 0.0).astype(BF16)
-    across = lax.broadcasted_iota(jnp.int32, (shots, cells), 1) == column_ref[...]
-    across = jnp.where(across, 1.0, 0.0).astype(BF16)
     blocks = cube_ref.shape[1] // TILE
     picked = []
     for block in range(blocks):
         rows = slice(block * TILE, (block + 1) * TILE)
         both = jnp.concatenate([cube_ref[0, rows, :], cube_ref[1, rows, :]], axis=0)
-        picked.append(dot(both, chosen).astype(BF16))
-        flat = nt_dot(across, both)
+        found = dot(both, chosen)
+        picked.append(found.astype(BF16))
+        flat = found.T
         columns = slice(block * PAIR, (block + 1) * PAIR)
         shots_ref[:shots, columns] = flat.astype(BF16)
         shots_ref[shots:, columns] = jnp.concatenate([flat[:, TILE:], -flat[:, :TILE]], axis=1).astype(BF16)
@@ -159,35 +197,7 @@
         ],
         name="sample",
         cost_estimate=cost(4),
-    )(cube, select[None, :], select[:, None])
-
-
-def beam_kernel(where_ref, steering_ref, shots_ref, out_ref):
-    vectors = steering_ref[0].reshape(shots_ref.shape[1], steering_ref.shape[3])
-    beams = dot(shots_ref[...], vectors)
-    out_ref[0] = jnp.sum(beams * beams, axis=0, keepdims=True)
-
-
-def local_energy(where, steering, shots, owned):
-    width = steering.shape[3]
-    near = lax.axis_size("snap") * owned // width
-    per = width // owned
-    grid_spec = pltpu.PrefetchScalarGridSpec(
-        num_scalar_prefetch=1,
-        grid=(near,),
-        in_specs=[
-            pl.BlockSpec((1, *steering.shape[1:]), lambda s, m: (m[0] // (per * near) * near + s, 0, 0, 0)),
-            pl.BlockSpec(shots.shape, lambda s, m: (0, 0)),
-        ],
-        out_specs=pl.BlockSpec((1, 1, width), lambda s, m: (s, 0, 0)),
-    )
-    return pl.pallas_call(
-        beam_kernel,
-        grid_spec=grid_spec,
-        out_shape=jax.ShapeDtypeStruct((near, 1, width), F32),
-        name="beams",
-        cost_estimate=cost(5),
-    )(where, steering, shots).reshape(near * per, owned)
+    )(cube, select[None, :])
 
 
 def swap(x, axis, mask):
@@ -227,8 +237,14 @@
 def gather_relative(x):
     snap, ang = lax.axis_size("snap"), lax.axis_size("ang")
     x = jnp.concatenate([x, swap(x, "snap", 1)], axis=0)
-    x = jnp.concatenate([x] + [swap(x, "snap", m) for m in range(2, snap, 2)], axis=0)
-    return [x] + [swap(x, "ang", m) for m in range(1, ang)]
+    parts = [x]
+    for m in range(2, snap, 2):
+        parts.append(swap(x, "snap", m))
+    x = jnp.concatenate(parts, axis=0)
+    parts = [x]
+    for m in range(1, ang):
+        parts.append(swap(x, "ang", m))
+    return parts
 
 
 def covariance_kernel(slots, table_ref, steering_ref, *refs):
@@ -393,10 +409,22 @@
 
 
 def step_kernel(
-    pairs, shots, where_ref, mine_ref, other_ref, steering_ref, high_ref, low_ref, out_ref, matrix, tile, inv_high, inv_low
+    pairs, shots, where_ref, mine_any, other_any, steering_any, high_any, low_any, out_ref,
+    mine_ref, other_ref, steering_ref, high_ref, low_ref, matrix, tile, inv_high, inv_low, copied
 ):
     order = matrix.shape[0]
     blocks = order // TILE
+    owned = steering_ref.shape[2]
+    per = steering_any.shape[3] // owned
+    column = pl.multiple_of((where_ref[0] % per) * owned, owned)
+    own_steering = steering_any.at[where_ref[0] // per, :, :, pl.ds(column, owned)]
+    sources = [mine_any, other_any, own_steering, high_any, low_any]
+    targets = [mine_ref, other_ref, steering_ref, high_ref, low_ref]
+    copies = [pltpu.make_async_copy(a, b, copied.at[n]) for n, (a, b) in enumerate(zip(sources, targets))]
+    for copy in copies:
+        copy.start()
+    for copy in copies[:2]:
+        copy.wait()
 
     def rows(i):
         return slice(i * TILE, (i + 1) * TILE)
@@ -472,7 +500,9 @@
                 weights += [weight, weight]
                 real = jnp.where(diagonal, 0.0, real)
             embed(store, i, j, real, imag)
-    vectors = steering_ref[0].reshape(2 * order, steering_ref.shape[3])
+    for copy in copies[2:]:
+        copy.wait()
+    vectors = steering_ref[...].reshape(2 * order, owned)
     wide = vectors.astype(F32)
     solved = dot(inv_high[...], vectors) + dot(inv_low[...], vectors) + jnp.concatenate(weights, axis=0) * wide
     norms = jnp.sum(solved * wide, axis=0, keepdims=True)
@@ -485,23 +515,24 @@
 def next_powers(where, mine, other, steering, sample, owned, pairs, shots):
     blocks = steering.shape[1]
     order = blocks * TILE
-    whole = lambda *shape: pl.BlockSpec(shape, lambda s, m: (0,) * len(shape))
+    square = pltpu.VMEM((2 * order, 2 * order), BF16)
+    operands = (mine, other, steering, *sample)
     grid_spec = pltpu.PrefetchScalarGridSpec(
         num_scalar_prefetch=1,
         grid=(1,),
-        in_specs=[
-            whole(*mine.shape),
-            whole(*other.shape),
-            own_block(steering.shape, owned),
-            whole(2 * order, 2 * order),
-            whole(2 * order, 2 * order),
-        ],
-        out_specs=whole(1, owned),
+        in_specs=[pl.BlockSpec(memory_space=pl.ANY)] * len(operands),
+        out_specs=pl.BlockSpec((1, owned), lambda s, m: (0, 0)),
         scratch_shapes=[
+            pltpu.VMEM(mine.shape, F32),
+            pltpu.VMEM(other.shape, F32),
+            pltpu.VMEM((blocks, PAIR, owned), BF16),
+            square,
+            square,
             pltpu.VMEM((order, 2 * order), F32),
             pltpu.VMEM((TILE, PAIR), F32),
-            pltpu.VMEM((2 * order, 2 * order), BF16),
-            pltpu.VMEM((2 * order, 2 * order), BF16),
+            square,
+            square,
+            pltpu.SemaphoreType.DMA((len(operands),)),
         ],
     )
     return pl.pallas_call(
@@ -509,9 +540,9 @@
         grid_spec=grid_spec,
         out_shape=jax.ShapeDtypeStruct((1, owned), F32),
         name="step",
-        cost_estimate=cost(35),
+        cost_estimate=cost(28),
         compiler_params=pltpu.CompilerParams(vmem_limit_bytes=56 * 1024 * 1024),
-    )(where, mine, other, steering, *sample)
+    )(where, *operands)
 
 
 def shards(cube, select, phases, jitter):
@@ -531,30 +562,32 @@
     ]
     table = jnp.concatenate([me[None], jnp.where(core == 0, flat[0], flat[1])])
 
-    steering = all_steering(phases, jitter, max(owned, WIDTH))
+    width = max(owned, WIDTH)
+    tables = angle_tables(phases, jitter, width // GV)
     every = [(a, b) for a in range(channels // TILE) for b in range(a + 1)]
     gram, rows = sample_terms(cube, select - snap_index * cube.shape[2], every)
-    piece = halve(halve(gram.reshape(-1, TILE), "snap", 0), "snap", 1)
-    steering, piece = lax.optimization_barrier((steering, piece))
-    energy = local_energy(where, steering, rows, owned)
-    powers = scatter_energy(energy) / float(shots * channels * channels)
-    for bit in range(2, snap_count.bit_length() - 1):
+    piece = halve(gram.reshape(-1, TILE), "snap", 0)
+    for bit in range(1, snap_count.bit_length() - 1):
         piece = halve(piece, "snap", bit)
+    steering, energy = fill_steering(where, tables, channels // TILE, owned, width, 0, shots=rows)
+    powers = scatter_energy(energy.reshape(snap_count, owned)) / float(shots * channels * channels)
+    for mask in range(1, ang_count):
+        (steering,) = fill_steering(
+            where, tables, channels // TILE, owned, width, mask, before=steering
+        )
+    gathered = gather_relative(powers)
 
     def iteration(gathered):
         mine = covariance_half(table, steering, gathered, slots)
         other = swap(mine, "snap", 1)
         return next_powers(where, mine, other, steering, sample, owned, pairs, float(shots))
 
-    gathered = gather_relative(powers)
     gathered, piece = lax.optimization_barrier((gathered, piece))
-
     others = []
     for m in range(2, snap_count, 2):
         others.append(swap(piece, "snap", m))
     both = jnp.concatenate([piece] + others, axis=0)
-    parts = [both, swap(both, "snap", 1)]
-    sample = spread(where, parts, every, 2 * channels)
+    sample = spread(where, [both, swap(both, "snap", 1)], every, 2 * channels)
     powers = iteration(gathered)
     return lax.fori_loop(1, ITERS, lambda _, powers: iteration(gather_relative(powers)), powers)[0]
 

time: 276 us -> 270 us (0.978)
  waiting for transfers between devices: 44.8 us -> 35.9 us
  Pallas kernels: 177 us -> 181 us
    ppermute x35, waiting for transfers between devices: 44.8 us -> 35.9 us  [swap(): return lax.ppermute(x, axis, [(i, i ^ mask) for i in range(size)])]
    pallas_call x2 -> x4, Pallas kernels: 23.1 us -> 30 us  [fill_steering(): pl.pallas_call(functools.partial(kernel, chunk_of), grid_spec=pltpu.Prefe...]
    pallas_call x3, Pallas kernels: 89.1 us -> 86.3 us  [next_powers(): pl.pallas_call(functools.partial(step_kernel, pairs, shots), grid_spec=gr...]
  transfers between devices with their start and end apart: 35 -> 35, of which waited for: 24 -> 19; matrix products, arithmetic and copies ran while one was open for 2% -> 2% of each run, Pallas kernels for 15% -> 20%
where the time goes in v1:
time: 270 us; the launch traced here: 269 us
  Pallas kernels  181 us (67%)
  starting transfers between devices  37.8 us (14%)
  waiting for transfers between devices  35.9 us (13%)
  local copies, waits for them, and re-layouts  6.86 us (3%)
  other arithmetic  6.36 us (2%)
    pallas_call x3, Pallas kernels, next_powers(): pl.pallas_call(functools.partial(step_kernel, pairs, shots), grid_spec=gr...  86.3 us
    pallas_call x3, Pallas kernels, covariance_half(): pl.pallas_call(functools.partial(covariance_kernel, slots), grid_spec=gri...  56.4 us
    ppermute x35, starting transfers between devices, swap(): return lax.ppermute(x, axis, [(i, i ^ mask) for i in range(size)])  37.8 us
    ppermute x35, waiting for transfers between devices, swap(): return lax.ppermute(x, axis, [(i, i ^ mask) for i in range(size)])  35.9 us
    pallas_call x4, Pallas kernels, fill_steering(): pl.pallas_call(functools.partial(kernel, chunk_of), grid_spec=pltpu.Prefe...  30 us
  transfers between devices with their start and end apart: 35, of which 19 were waited for; matrix products, arithmetic and copies ran while one was open for 2% of the time, Pallas kernels for 20%

profile of v1, /device:TPU:0, one launch (start us, length us, event | category | flops | bytes accessed | tf_op | source)
XLA Modules:
  0.0 268.8 jit_solution(16834242485265928474)
XLA Ops:
  1.2 3.9 %sample.1 = (f32[20,128,128]{2,1,0:T(8,128)}, bf16[256,1024]{1,0:T(8,128)(2,1)}) custom-call(bf16[2,512,1024]{2,1,0:T(8,128)(2,1)} %cube_ref.1, s32[1,128]{1,0:T(1,128)} %subtract_bitcast_fusion.select_ref), custom_call_target="tpu_custom_call" | custom-call | flops 4000000000 | bytes 12000000 | tf_op jit(solution)/shard_map/sample/pallas_call | solution.py:192
  7.6 3.7 %fusion = (f32[3,512,128]{2,1,0:T(8,128)}, f32[3,512,128]{2,1,0:T(8,128)}) fusion(f32[1,512,128]{2,1,0:T(8,128)S(1)} %stack_broadcast_in_dim.8, f32[1,512,128]{2,1,0:T(8,128)S(1)} %multiply_add_fusion, f32[1,512,128]{2,1,0:T(8,128)S(1)} %multiply_multiply_fusion), kind=kLoop, calls=%fused_computation.2 | loop fusion | flops 393216 | bytes 2359296 | tf_op jit(solution)/shard_map/sin | solution.py:86
  11.3 9.8 %near_steering.1 = (bf16[8,4,256,2048]{3,2,1,0:T(8,128)(2,1)}, f32[2,1,2048]{2,1,0:T(1,128)}) custom-call(s32[2]{0:T(128)S(1)} %pad_add_fusion.where_ref, f32[3,512,128]{2,1,0:T(8,128)} %get-tuple-element.80.real_ref, f32[3,512,128]{2,1,0:T(8,128)} %get-tuple-element.79.imag_ref, bf16[256,1024]{1,0:T(8,128)(2,1)} %get-tuple-element.53.shots_ref), custom_call_target="tpu_custom_call" | custom-call | flops 8000000000 | bytes 24000000 | tf_op jit(solution)/shard_map/near_steering/pallas_call | solution.py:152
  22.1 6.7 %far_steering.3.before_ref = bf16[8,4,256,2048]{3,2,1,0:T(8,128)(2,1)} custom-call(s32[2]{0:T(128)S(1)} %pad_add_fusion.where_ref, f32[3,512,128]{2,1,0:T(8,128)} %get-tuple-element.80.real_ref, f32[3,512,128]{2,1,0:T(8,128)} %get-tuple-element.79.imag_ref, bf16[8,4,256,2048]{3,2,1,0:T(8,128)(2,1)} %get-tuple-element.54.before_ref), custom_call_target="tpu_custom_call", output_to_operand_aliasing={{}: (3, {})} | custom-call | flops 5000000000 | bytes 15000000 | tf_op jit(solution)/shard_map/far_steering/pallas_call | solution.py:152
  28.8 3.1 %collective-permute-start.9 = (f32[1,512]{1,0:T(1,128)S(1)}, f32[1,512]{1,0:T(1,128)S(1)}, u32[]{:S(2)}, u32[]{:S(2)}) collective-permute-start(f32[1,512]{1,0:T(1,128)S(1)} %get-tuple-element.83), channel_id=1, source_target_pairs={{0,2},{1,3},{2,0},{3,1},{4,6},{5,7},{6,4},{7,5},{8,10},{9,11},{10,... | collective-permute-start | bytes 6152 | tf_op jit(solution)/shard_map/ppermute | solution.py:205
  31.9 2.5 collective-permute-start.11
  34.5 6.7 %far_steering.4.before_ref = bf16[8,4,256,2048]{3,2,1,0:T(8,128)(2,1)} custom-call(s32[2]{0:T(128)S(1)} %pad_add_fusion.where_ref, f32[3,512,128]{2,1,0:T(8,128)} %get-tuple-element.80.real_ref, f32[3,512,128]{2,1,0:T(8,128)} %get-tuple-element.79.imag_ref, bf16[8,4,256,2048]{3,2,1,0:T(8,128)(2,1)} %far_steering.3.before_ref), custom_call_target="tpu_custom_call", output_to_operand_aliasing={{}: (3, {})} | custom-call | flops 5000000000 | bytes 15000000 | tf_op jit(solution)/shard_map/far_steering/pallas_call | solution.py:152
  41.5 1.9 collective-permute-start.20
  43.4 6.7 %far_steering.5.steering_ref.steering_any = bf16[8,4,256,2048]{3,2,1,0:T(8,128)(2,1)} custom-call(s32[2]{0:T(128)S(1)} %pad_add_fusion.where_ref, f32[3,512,128]{2,1,0:T(8,128)} %get-tuple-element.80.real_ref, f32[3,512,128]{2,1,0:T(8,128)} %get-tuple-element.79.imag_ref, ...), custom_call_target="tpu_custom_call", output_to_operand_aliasing={{}: (3, {})} | custom-call | flops 5000000000 | bytes 15000000 | tf_op jit(solution)/shard_map/far_steering/pallas_call | solution.py:152
  50.1 2.5 collective-permute-start.15
  52.7 1.9 collective-permute-start.13
  57.2 2.4 collective-permute-start.18
  60.8 3.7 %collective-permute-done.21 = f32[320,128]{1,0:T(8,128)S(1)} collective-permute-done((f32[320,128]{1,0:T(8,128)S(1)}, f32[320,128]{1,0:T(8,128)S(1)}, u32[]{:S(2)}, u32[]{:S(2)}) %collective-permute-start.21) | collective-permute-done | bytes 163872 | tf_op jit(solution)/shard_map/ppermute | solution.py:205
  65.1 2.5 collective-permute-start.25
  68.2 3.0 %collective-permute-done.23 = f32[320,128]{1,0:T(8,128)S(1)} collective-permute-done((f32[320,128]{1,0:T(8,128)S(1)}, f32[320,128]{1,0:T(8,128)S(1)}, u32[]{:S(2)}, u32[]{:S(2)}) %collective-permute-start.23) | collective-permute-done | bytes 163872 | tf_op jit(solution)/shard_map/ppermute | solution.py:205
  71.2 11.3 %collective-permute-done.24 = f32[320,128]{1,0:T(8,128)S(1)} collective-permute-done((f32[320,128]{1,0:T(8,128)S(1)}, f32[320,128]{1,0:T(8,128)S(1)}, u32[]{:S(2)}, u32[]{:S(2)}) %collective-permute-start.24) | collective-permute-done | bytes 163872 | tf_op jit(solution)/shard_map/ppermute | solution.py:205
  82.7 18.7 %covariance.2.mine_any = f32[10,128,128]{2,1,0:T(8,128)} custom-call(s32[8]{0:T(128)S(1)} %pad_add_fusion.1.table_ref, bf16[8,4,256,2048]{3,2,1,0:T(8,128)(2,1)} %far_steering.5.steering_ref.steering_any, f32[8,512]{1,0:T(8,128)} %copy-done.4, f32[8,512]{1,0:T(8,128)} %copy-done.13, f32[8,512]{1,0:T(8,128)} %copy-done.12, f32[8,512]{1,0:T(8,128)} %copy-done.11), custom_call_target="tpu_custom_call" | custom-call | flops 16999999488 | bytes 51000000 | tf_op jit(solution)/shard_map/covariance/pallas_call | solution.py:297
  102.8 4.6 %spread.1 = (bf16[1024,1024]{1,0:T(8,128)(2,1)}, bf16[1024,1024]{1,0:T(8,128)(2,1)}) custom-call(s32[2]{0:T(128)S(1)} %pad_add_fusion.where_ref, f32[1280,128]{1,0:T(8,128)} %copy-done.3, f32[1280,128]{1,0:T(8,128)} %copy-done.8), custom_call_target="tpu_custom_call" | custom-call | flops 3000000000 | bytes 9000000 | tf_op jit(solution)/shard_map/spread/pallas_call | solution.py:339
  108.2 28.9 %step.2 = f32[1,512]{1,0:T(1,128)S(1)} custom-call(s32[2]{0:T(128)S(1)} %pad_add_fusion.where_ref, f32[10,128,128]{2,1,0:T(8,128)} %covariance.2.mine_any, f32[10,128,128]{2,1,0:T(8,128)} %copy-done.9, bf16[8,4,256,2048]{3,2,1,0:T(8,128)(2,1)} %far_steering.5.steering_ref.steering_any, bf16[1024,1024]{1,0:T(8,128)(2,1)} %get-tuple-element.139.high_any, ...), custom_call_target="tpu_custom_call" | custom-call | flops 28000000000 | bytes 84000000 | tf_op jit(solution)/shard_map/step/pallas_call | solution.py:538
  137.1 131.1 %while.10 = (s32[]{:T(128)}, f32[1,512]{1,0:T(1,128)S(1)}, s32[8]{0:T(128)S(1)}, bf16[8,4,256,2048]{3,2,1,0:T(8,128)(2,1)}, s32[2]{0:T(128)S(1)}, /*index=5*/bf1...) while((s32[]{:T(128)}, f32[1,512]{1,0:T(1,128)S(1)}, s32[8]{0:T(128)S(1)}, ...), condition=%wide.region_1.2_spmd, body=%wide.region_0.1_spmd.sunk | while | flops 44999999488 | bytes 149189120 | solution.py:592
  138.6 2.5 collective-permute-start.3
  141.0 2.0 collective-permute-start.1
  145.6 2.5 collective-permute-start.6
  152.9 18.8 %covariance.3.mine_any = f32[10,128,128]{2,1,0:T(8,128)} custom-call(s32[8]{0:T(128)S(1)} %get-tuple-element.152.table_ref, bf16[8,4,256,2048]{3,2,1,0:T(8,128)(2,1)} %get-tuple-element.153.steering_ref.steering_any, f32[8,512]{1,0:T(8,128)} %copy-done.1, f32[8,512]{1,0:T(8,128)} %copy-done.16, f32[8,512]{1,0:T(8,128)} %copy-done.15, f32[8,512]{1,0:T(8,128)} %copy-done.14), custom_call_target="tpu_custom_call" | custom-call | flops 16999999488 | bytes 51000000 | tf_op jit(solution)/shard_map/while/body/eval_jaxpr/covariance/pallas_call | solution.py:297
  171.7 2.3 collective-permute-done.7.other_any
  174.8 28.7 %step.3 = f32[1,512]{1,0:T(1,128)S(1)} custom-call(s32[2]{0:T(128)S(1)} %get-tuple-element.154.where_ref, f32[10,128,128]{2,1,0:T(8,128)} %covariance.3.mine_any, f32[10,128,128]{2,1,0:T(8,128)} %copy-done.10, bf16[8,4,256,2048]{3,2,1,0:T(8,128)(2,1)} %get-tuple-element.153.steering_ref.steering_any, bf16[1024,1024]{1,0:T(8,128)(2,1)S(1)} %copy-done.18, ...), custom_call_target="tpu_custom_call" | custom-call | flops 28000000000 | bytes 84000000 | tf_op jit(solution)/shard_map/while/body/eval_jaxpr/step/pallas_call | solution.py:538
  204.8 1.5 collective-permute-start.3
  207.4 1.8 collective-permute-start.1
  211.0 1.6 collective-permute-start.6
  217.5 18.8 %covariance.3.mine_any = f32[10,128,128]{2,1,0:T(8,128)} custom-call(s32[8]{0:T(128)S(1)} %get-tuple-element.152.table_ref, bf16[8,4,256,2048]{3,2,1,0:T(8,128)(2,1)} %get-tuple-element.153.steering_ref.steering_any, f32[8,512]{1,0:T(8,128)} %copy-done.1, f32[8,512]{1,0:T(8,128)} %copy-done.16, f32[8,512]{1,0:T(8,128)} %copy-done.15, f32[8,512]{1,0:T(8,128)} %copy-done.14), custom_call_target="tpu_custom_call" | custom-call | flops 16999999488 | bytes 51000000 | tf_op jit(solution)/shard_map/while/body/eval_jaxpr/covariance/pallas_call | solution.py:297
  236.3 2.3 collective-permute-done.7.other_any
  239.5 28.7 %step.3 = f32[1,512]{1,0:T(1,128)S(1)} custom-call(s32[2]{0:T(128)S(1)} %get-tuple-element.154.where_ref, f32[10,128,128]{2,1,0:T(8,128)} %covariance.3.mine_any, f32[10,128,128]{2,1,0:T(8,128)} %copy-done.10, bf16[8,4,256,2048]{3,2,1,0:T(8,128)(2,1)} %get-tuple-element.153.steering_ref.steering_any, bf16[1024,1024]{1,0:T(8,128)(2,1)S(1)} %copy-done.18, ...), custom_call_target="tpu_custom_call" | custom-call | flops 28000000000 | bytes 84000000 | tf_op jit(solution)/shard_map/while/body/eval_jaxpr/step/pallas_call | solution.py:538
  (139 shorter events, 32.0 us)
Async XLA Ops:
  6.3 35.1 %collective-permute-start.19 = (f32[1280,128]{1,0:T(8,128)S(1)}, f32[1280,128]{1,0:T(8,128)S(1)}, u32[]{:S(2)}, u32[]{:S(2)}) collective-permute-start(f32[1280,128]{1,0:T(8,128)S(1)} %constant_dynamic-slice_fusion.2), channel_id=1, source_target_pairs={{0,1},{1,0},{2,3},{3,2},{4,5},{5,4},{6,7},{7,6},{8,9},{9,8},{10,11... | collective-permute-start | bytes 1966088 | tf_op jit(solution)/shard_map/ppermute | solution.py:205
  22.0 6.8 %collective-permute-start.8 = (f32[4,512]{1,0:T(4,128)S(1)}, f32[4,512]{1,0:T(4,128)S(1)}, u32[]{:S(2)}, u32[]{:S(2)}) collective-permute-start(f32[4,512]{1,0:T(4,128)S(1)} %bitcast.19), channel_id=1, source_target_pairs={{0,1},{1,0},{2,3},{3,2},{4,5},{5,4},{6,7},{7,6},{8,9},{9,8},{10,11... | collective-permute-start | bytes 24584 | tf_op jit(solution)/shard_map/ppermute | solution.py:205
  28.8 12.4 %collective-permute-start.9 = (f32[1,512]{1,0:T(1,128)S(1)}, f32[1,512]{1,0:T(1,128)S(1)}, u32[]{:S(2)}, u32[]{:S(2)}) collective-permute-start(f32[1,512]{1,0:T(1,128)S(1)} %get-tuple-element.83), channel_id=1, source_target_pairs={{0,2},{1,3},{2,0},{3,1},{4,6},{5,7},{6,4},{7,5},{8,10},{9,11},{10,... | collective-permute-start | bytes 6152 | tf_op jit(solution)/shard_map/ppermute | solution.py:205
  31.9 9.3 %collective-permute-start.11 = (f32[1,512]{1,0:T(1,128)S(1)}, f32[1,512]{1,0:T(1,128)S(1)}, u32[]{:S(2)}, u32[]{:S(2)}) collective-permute-start(f32[1,512]{1,0:T(1,128)S(1)} %get-tuple-element.84), channel_id=1, source_target_pairs={{0,6},{1,7},{2,4},{3,5},{4,2},{5,3},{6,0},{7,1},{8,14},{9,15},{10,... | collective-permute-start | bytes 6152 | tf_op jit(solution)/shard_map/ppermute | solution.py:205
  34.4 6.9 %collective-permute-start.10 = (f32[1,512]{1,0:T(1,128)S(1)}, f32[1,512]{1,0:T(1,128)S(1)}, u32[]{:S(2)}, u32[]{:S(2)}) collective-permute-start(f32[1,512]{1,0:T(1,128)S(1)} %get-tuple-element.85), channel_id=1, source_target_pairs={{0,4},{1,5},{2,6},{3,7},{4,0},{5,1},{6,2},{7,3},{8,12},{9,13},{10,... | collective-permute-start | bytes 6152 | tf_op jit(solution)/shard_map/ppermute | solution.py:205
  41.3 8.8 %collective-permute-start.12 = (f32[1,512]{1,0:T(1,128)S(1)}, f32[1,512]{1,0:T(1,128)S(1)}, u32[]{:S(2)}, u32[]{:S(2)}) collective-permute-start(f32[1,512]{1,0:T(1,128)S(1)} %fusion.18), channel_id=1, source_target_pairs={{0,1},{1,0},{2,3},{3,2},{4,5},{5,4},{6,7},{7,6},{8,9},{9,8},{10,11... | collective-permute-start | bytes 6152 | tf_op jit(solution)/shard_map/ppermute | solution.py:205
  41.5 13.1 %collective-permute-start.20 = (f32[640,128]{1,0:T(8,128)S(1)}, f32[640,128]{1,0:T(8,128)S(1)}, u32[]{:S(2)}, u32[]{:S(2)}) collective-permute-start(f32[640,128]{1,0:T(8,128)S(1)} %constant_dynamic-slice_fusion.1), channel_id=1, source_target_pairs={{0,2},{1,3},{2,0},{3,1},{4,6},{5,7},{6,4},{7,5},{8,10},{9,11},{10,... | collective-permute-start | bytes 983048 | tf_op jit(solution)/shard_map/ppermute | solution.py:205
  50.1 5.6 %collective-permute-start.15 = (f32[2,512]{1,0:T(2,128)S(1)}, f32[2,512]{1,0:T(2,128)S(1)}, u32[]{:S(2)}, u32[]{:S(2)}) collective-permute-start(f32[2,512]{1,0:T(2,128)S(1)} %pad_maximum_fusion.2), channel_id=1, source_target_pairs={{0,6},{1,7},{2,4},{3,5},{4,2},{5,3},{6,0},{7,1},{8,14},{9,15},{10,... | collective-permute-start | bytes 12296 | tf_op jit(solution)/shard_map/ppermute | solution.py:205
  52.7 4.5 %collective-permute-start.14 = (f32[2,512]{1,0:T(2,128)S(1)}, f32[2,512]{1,0:T(2,128)S(1)}, u32[]{:S(2)}, u32[]{:S(2)}) collective-permute-start(f32[2,512]{1,0:T(2,128)S(1)} %pad_maximum_fusion.2), channel_id=1, source_target_pairs={{0,4},{1,5},{2,6},{3,7},{4,0},{5,1},{6,2},{7,3},{8,12},{9,13},{10,... | collective-permute-start | bytes 12296 | tf_op jit(solution)/shard_map/ppermute | solution.py:205
  52.7 4.5 %collective-permute-start.13 = (f32[2,512]{1,0:T(2,128)S(1)}, f32[2,512]{1,0:T(2,128)S(1)}, u32[]{:S(2)}, u32[]{:S(2)}) collective-permute-start(f32[2,512]{1,0:T(2,128)S(1)} %pad_maximum_fusion.2), channel_id=1, source_target_pairs={{0,2},{1,3},{2,0},{3,1},{4,6},{5,7},{6,4},{7,5},{8,10},{9,11},{10,... | collective-permute-start | bytes 12296 | tf_op jit(solution)/shard_map/ppermute | solution.py:205
  54.7 9.8 %collective-permute-start.21 = (f32[320,128]{1,0:T(8,128)S(1)}, f32[320,128]{1,0:T(8,128)S(1)}, u32[]{:S(2)}, u32[]{:S(2)}) collective-permute-start(f32[320,128]{1,0:T(8,128)S(1)} %constant_dynamic-slice_fusion), channel_id=1, source_target_pairs={{0,4},{1,5},{2,6},{3,7},{4,0},{5,1},{6,2},{7,3},{8,12},{9,13},{10,... | collective-permute-start | bytes 491528 | tf_op jit(solution)/shard_map/ppermute | solution.py:205
  57.2 7.2 %collective-permute-start.18 = (f32[8,512]{1,0:T(8,128)S(1)}, f32[8,512]{1,0:T(8,128)S(1)}, u32[]{:S(2)}, u32[]{:S(2)}) collective-permute-start(f32[8,512]{1,0:T(8,128)S(1)} %concatenate.22.refs_0_), channel_id=1, source_target_pairs={{0,24},{8,16},{16,8},{24,0},{1,25},{9,17},{17,9},{25,1},{2,26},{10... | collective-permute-start | bytes 49160 | tf_op jit(solution)/shard_map/ppermute | solution.py:205
  59.7 4.8 %collective-permute-start.17 = (f32[8,512]{1,0:T(8,128)S(1)}, f32[8,512]{1,0:T(8,128)S(1)}, u32[]{:S(2)}, u32[]{:S(2)}) collective-permute-start(f32[8,512]{1,0:T(8,128)S(1)} %concatenate.22.refs_0_), channel_id=1, source_target_pairs={{0,16},{8,24},{16,0},{24,8},{1,17},{9,25},{17,1},{25,9},{2,18},{10... | collective-permute-start | bytes 49160 | tf_op jit(solution)/shard_map/ppermute | solution.py:205
  60.2 4.3 %collective-permute-start.16 = (f32[8,512]{1,0:T(8,128)S(1)}, f32[8,512]{1,0:T(8,128)S(1)}, u32[]{:S(2)}, u32[]{:S(2)}) collective-permute-start(f32[8,512]{1,0:T(8,128)S(1)} %concatenate.22.refs_0_), channel_id=1, source_target_pairs={{0,8},{8,0},{16,24},{24,16},{1,9},{9,1},{17,25},{25,17},{2,10},{10... | collective-permute-start | bytes 49160 | tf_op jit(solution)/shard_map/ppermute | solution.py:205
  64.5 6.6 %collective-permute-start.23 = (f32[320,128]{1,0:T(8,128)S(1)}, f32[320,128]{1,0:T(8,128)S(1)}, u32[]{:S(2)}, u32[]{:S(2)}) collective-permute-start(f32[320,128]{1,0:T(8,128)S(1)} %dynamic-slice_add_fusion.2), channel_id=1, source_target_pairs={{0,2},{1,3},{2,0},{3,1},{4,6},{5,7},{6,4},{7,5},{8,10},{9,11},{10,... | collective-permute-start | bytes 491528 | tf_op jit(solution)/shard_map/ppermute | solution.py:205
  65.1 17.5 %collective-permute-start.25 = (f32[320,128]{1,0:T(8,128)S(1)}, f32[320,128]{1,0:T(8,128)S(1)}, u32[]{:S(2)}, u32[]{:S(2)}) collective-permute-start(f32[320,128]{1,0:T(8,128)S(1)} %dynamic-slice_add_fusion.2), channel_id=1, source_target_pairs={{0,6},{1,7},{2,4},{3,5},{4,2},{5,3},{6,0},{7,1},{8,14},{9,15},{10,... | collective-permute-start | bytes 491528 | tf_op jit(solution)/shard_map/ppermute | solution.py:205
  67.5 15.0 %collective-permute-start.24 = (f32[320,128]{1,0:T(8,128)S(1)}, f32[320,128]{1,0:T(8,128)S(1)}, u32[]{:S(2)}, u32[]{:S(2)}) collective-permute-start(f32[320,128]{1,0:T(8,128)S(1)} %dynamic-slice_add_fusion.2), channel_id=1, source_target_pairs={{0,4},{1,5},{2,6},{3,7},{4,0},{5,1},{6,2},{7,3},{8,12},{9,13},{10,... | collective-permute-start | bytes 491528 | tf_op jit(solution)/shard_map/ppermute | solution.py:205
  82.6 19.3 %collective-permute-start.26 = (f32[1280,128]{1,0:T(8,128)S(1)}, f32[1280,128]{1,0:T(8,128)S(1)}, u32[]{:S(2)}, u32[]{:S(2)}) collective-permute-start(f32[1280,128]{1,0:T(8,128)S(1)} %constant_dynamic-update-slice_fusion.refs_0_), channel_id=1, source_target_pairs={{0,1},{1,0},{2,3},{3,2},{4,5},{5,4},{6,7},{7,6},{8,9},{9,8},{10,11... | collective-permute-start | bytes 1966088 | tf_op jit(solution)/shard_map/ppermute | solution.py:205
  101.4 5.9 %collective-permute-start.22 = (f32[10,128,128]{2,1,0:T(8,128)}, f32[10,128,128]{2,1,0:T(8,128)S(1)}, u32[]{:S(2)}, u32[]{:S(2)}) collective-permute-start(f32[10,128,128]{2,1,0:T(8,128)} %covariance.2.mine_any), channel_id=1, source_target_pairs={{0,1},{1,0},{2,3},{3,2},{4,5},{5,4},{6,7},{7,6},{8,9},{9,8},{10,11... | collective-permute-start | bytes 1966088 | tf_op jit(solution)/shard_map/ppermute | solution.py:205
  138.6 5.5 %collective-permute-start.3 = (f32[2,512]{1,0:T(2,128)S(1)}, f32[2,512]{1,0:T(2,128)S(1)}, u32[]{:S(2)}, u32[]{:S(2)}) collective-permute-start(f32[2,512]{1,0:T(2,128)S(1)} %pad_maximum_fusion.4), channel_id=1, source_target_pairs={{0,6},{1,7},{2,4},{3,5},{4,2},{5,3},{6,0},{7,1},{8,14},{9,15},{10,... | collective-permute-start | bytes 12296 | tf_op jit(solution)/shard_map/while/body/eval_jaxpr/ppermute | solution.py:205
  141.0 4.5 %collective-permute-start.2 = (f32[2,512]{1,0:T(2,128)S(1)}, f32[2,512]{1,0:T(2,128)S(1)}, u32[]{:S(2)}, u32[]{:S(2)}) collective-permute-start(f32[2,512]{1,0:T(2,128)S(1)} %pad_maximum_fusion.4), channel_id=1, source_target_pairs={{0,4},{1,5},{2,6},{3,7},{4,0},{5,1},{6,2},{7,3},{8,12},{9,13},{10,... | collective-permute-start | bytes 12296 | tf_op jit(solution)/shard_map/while/body/eval_jaxpr/ppermute | solution.py:205
  141.0 4.5 %collective-permute-start.1 = (f32[2,512]{1,0:T(2,128)S(1)}, f32[2,512]{1,0:T(2,128)S(1)}, u32[]{:S(2)}, u32[]{:S(2)}) collective-permute-start(f32[2,512]{1,0:T(2,128)S(1)} %pad_maximum_fusion.4), channel_id=1, source_target_pairs={{0,2},{1,3},{2,0},{3,1},{4,6},{5,7},{6,4},{7,5},{8,10},{9,11},{10,... | collective-permute-start | bytes 12296 | tf_op jit(solution)/shard_map/while/body/eval_jaxpr/ppermute | solution.py:205
  145.6 4.8 %collective-permute-start.6 = (f32[8,512]{1,0:T(8,128)S(1)}, f32[8,512]{1,0:T(8,128)S(1)}, u32[]{:S(2)}, u32[]{:S(2)}) collective-permute-start(f32[8,512]{1,0:T(8,128)S(1)} %concatenate.25.refs_0_), channel_id=1, source_target_pairs={{0,24},{8,16},{16,8},{24,0},{1,25},{9,17},{17,9},{25,1},{2,26},{10... | collective-permute-start | bytes 49160 | tf_op jit(solution)/shard_map/while/body/eval_jaxpr/ppermute | solution.py:205
  148.0 3.7 %collective-permute-start.5 = (f32[8,512]{1,0:T(8,128)S(1)}, f32[8,512]{1,0:T(8,128)S(1)}, u32[]{:S(2)}, u32[]{:S(2)}) collective-permute-start(f32[8,512]{1,0:T(8,128)S(1)} %concatenate.25.refs_0_), channel_id=1, source_target_pairs={{0,16},{8,24},{16,0},{24,8},{1,17},{9,25},{17,1},{25,9},{2,18},{10... | collective-permute-start | bytes 49160 | tf_op jit(solution)/shard_map/while/body/eval_jaxpr/ppermute | solution.py:205
  148.5 3.7 %collective-permute-start.4 = (f32[8,512]{1,0:T(8,128)S(1)}, f32[8,512]{1,0:T(8,128)S(1)}, u32[]{:S(2)}, u32[]{:S(2)}) collective-permute-start(f32[8,512]{1,0:T(8,128)S(1)} %concatenate.25.refs_0_), channel_id=1, source_target_pairs={{0,8},{8,0},{16,24},{24,16},{1,9},{9,1},{17,25},{25,17},{2,10},{10... | collective-permute-start | bytes 49160 | tf_op jit(solution)/shard_map/while/body/eval_jaxpr/ppermute | solution.py:205
  171.7 2.3 collective-permute-start.7
  204.8 5.5 %collective-permute-start.3 = (f32[2,512]{1,0:T(2,128)S(1)}, f32[2,512]{1,0:T(2,128)S(1)}, u32[]{:S(2)}, u32[]{:S(2)}) collective-permute-start(f32[2,512]{1,0:T(2,128)S(1)} %pad_maximum_fusion.4), channel_id=1, source_target_pairs={{0,6},{1,7},{2,4},{3,5},{4,2},{5,3},{6,0},{7,1},{8,14},{9,15},{10,... | collective-permute-start | bytes 12296 | tf_op jit(solution)/shard_map/while/body/eval_jaxpr/ppermute | solution.py:205
  206.3 4.5 %collective-permute-start.2 = (f32[2,512]{1,0:T(2,128)S(1)}, f32[2,512]{1,0:T(2,128)S(1)}, u32[]{:S(2)}, u32[]{:S(2)}) collective-permute-start(f32[2,512]{1,0:T(2,128)S(1)} %pad_maximum_fusion.4), channel_id=1, source_target_pairs={{0,4},{1,5},{2,6},{3,7},{4,0},{5,1},{6,2},{7,3},{8,12},{9,13},{10,... | collective-permute-start | bytes 12296 | tf_op jit(solution)/shard_map/while/body/eval_jaxpr/ppermute | solution.py:205
  207.4 3.6 %collective-permute-start.1 = (f32[2,512]{1,0:T(2,128)S(1)}, f32[2,512]{1,0:T(2,128)S(1)}, u32[]{:S(2)}, u32[]{:S(2)}) collective-permute-start(f32[2,512]{1,0:T(2,128)S(1)} %pad_maximum_fusion.4), channel_id=1, source_target_pairs={{0,2},{1,3},{2,0},{3,1},{4,6},{5,7},{6,4},{7,5},{8,10},{9,11},{10,... | collective-permute-start | bytes 12296 | tf_op jit(solution)/shard_map/while/body/eval_jaxpr/ppermute | solution.py:205
  211.0 4.7 %collective-permute-start.6 = (f32[8,512]{1,0:T(8,128)S(1)}, f32[8,512]{1,0:T(8,128)S(1)}, u32[]{:S(2)}, u32[]{:S(2)}) collective-permute-start(f32[8,512]{1,0:T(8,128)S(1)} %concatenate.25.refs_0_), channel_id=1, source_target_pairs={{0,24},{8,16},{16,8},{24,0},{1,25},{9,17},{17,9},{25,1},{2,26},{10... | collective-permute-start | bytes 49160 | tf_op jit(solution)/shard_map/while/body/eval_jaxpr/ppermute | solution.py:205
  212.7 3.7 %collective-permute-start.5 = (f32[8,512]{1,0:T(8,128)S(1)}, f32[8,512]{1,0:T(8,128)S(1)}, u32[]{:S(2)}, u32[]{:S(2)}) collective-permute-start(f32[8,512]{1,0:T(8,128)S(1)} %concatenate.25.refs_0_), channel_id=1, source_target_pairs={{0,16},{8,24},{16,0},{24,8},{1,17},{9,25},{17,1},{25,9},{2,18},{10... | collective-permute-start | bytes 49160 | tf_op jit(solution)/shard_map/while/body/eval_jaxpr/ppermute | solution.py:205
  213.2 3.7 %collective-permute-start.4 = (f32[8,512]{1,0:T(8,128)S(1)}, f32[8,512]{1,0:T(8,128)S(1)}, u32[]{:S(2)}, u32[]{:S(2)}) collective-permute-start(f32[8,512]{1,0:T(8,128)S(1)} %concatenate.25.refs_0_), channel_id=1, source_target_pairs={{0,8},{8,0},{16,24},{24,16},{1,9},{9,1},{17,25},{25,17},{2,10},{10... | collective-permute-start | bytes 49160 | tf_op jit(solution)/shard_map/while/body/eval_jaxpr/ppermute | solution.py:205
  (28 other events, 216.3 us)

commit v2 on v1

--- a/solution.py
+++ b/solution.py
@@ -77,18 +77,18 @@
     position_y = (channel // RX).astype(F32) + jitter[1]
     offsets = jnp.broadcast_to(phases[:, None], (phases.shape[0], RX)).reshape(channels).astype(F32)
     lane = jnp.arange(GV, dtype=jnp.int32)
-    row_angle = (2 * steps * lane - GU).astype(F32) / GU
+    row_angle = jnp.where(lane == GV - 1, 2.0, (2 * steps * lane - GU).astype(F32)) / GU
     col_angle = (2 * lane - GV).astype(F32) / GV
-    start = math.pi * (position_x[:, None] * row_angle[None, :])
+    row = math.pi * (position_x[:, None] * row_angle[None, :])
     col = math.pi * (position_y[:, None] * col_angle[None, :]) + 2.0 * math.pi / Q * offsets[:, None]
-    turn = jnp.broadcast_to((math.pi * 2.0 / GU) * position_x[:, None], (channels, GV))
-    angles = jnp.stack([start, col, turn])
+    angles = jnp.stack([row, col])
     return jnp.cos(angles), jnp.sin(angles)
 
 
 def fill_blocks(chunk, first, real_ref, imag_ref, out_ref):
     steps = out_ref.shape[3] // GV
     spot = jnp.full((TILE, GV), chunk, jnp.int32)
+    turn = jnp.full((TILE, GV), GV - 1, jnp.int32)
 
     def block(b, _):
         rows = pl.ds(pl.multiple_of((first + b) * TILE, TILE), TILE)
@@ -96,7 +96,7 @@
         across_real, across_imag = real_ref[1, rows, :], imag_ref[1, rows, :]
         real = across_real * first_real - across_imag * first_imag
         imag = across_real * first_imag + across_imag * first_real
-        by_real, by_imag = real_ref[2, rows, :], imag_ref[2, rows, :]
+        by_real, by_imag = take(real_ref[0, rows, :], turn), take(imag_ref[0, rows, :], turn)
         for step in range(steps):
             if step:
                 real, imag = real * by_real - imag * by_imag, real * by_imag + imag * by_real
@@ -165,7 +165,7 @@
     )(where, *tables, last)
 
 
-def sample_kernel(pairs, cube_ref, select_ref, gram_ref, shots_ref):
+def sample_kernel(pairs, where_ref, cube_ref, select_ref, keep_ref, give_ref, shots_ref, gram_ref):
     cells = cube_ref.shape[2]
     shots = select_ref.shape[1]
     chosen = lax.broadcasted_iota(jnp.int32, (cells, shots), 0) == select_ref[...]
@@ -185,19 +185,32 @@
         real, imag = complex_block(nt_dot(picked[a], picked[b]))
         gram_ref[2 * index] = real
         gram_ref[2 * index + 1] = imag
-
-
-def sample_terms(cube, select, pairs):
+    keep_ref[...] = gram_ref[pl.ds(where_ref[1] * len(pairs), len(pairs))]
+    give_ref[...] = gram_ref[pl.ds((1 - where_ref[1]) * len(pairs), len(pairs))]
+
+
+def sample_terms(where, cube, select, pairs):
     shots = select.shape[0]
+    whole = lambda *shape: pl.BlockSpec(shape, lambda s, m: (0,) * len(shape))
+    half = (len(pairs), TILE, TILE)
+    turned = (2 * shots, 2 * cube.shape[1])
     return pl.pallas_call(
         functools.partial(sample_kernel, pairs),
+        grid_spec=pltpu.PrefetchScalarGridSpec(
+            num_scalar_prefetch=1,
+            grid=(1,),
+            in_specs=[whole(*cube.shape), whole(1, shots)],
+            out_specs=[whole(*half), whole(*half), whole(*turned)],
+            scratch_shapes=[pltpu.VMEM((2 * len(pairs), TILE, TILE), F32)],
+        ),
         out_shape=[
-            jax.ShapeDtypeStruct((2 * len(pairs), TILE, TILE), F32),
-            jax.ShapeDtypeStruct((2 * shots, 2 * cube.shape[1]), BF16),
+            jax.ShapeDtypeStruct(half, F32),
+            jax.ShapeDtypeStruct(half, F32),
+            jax.ShapeDtypeStruct(turned, BF16),
         ],
         name="sample",
         cost_estimate=cost(4),
-    )(cube, select[None, :])
+    )(where, cube, select[None, :])
 
 
 def swap(x, axis, mask):
@@ -303,14 +316,6 @@
     )(table, steering, *powers)
 
 
-def embed(store, i, j, real, imag):
-    top, left = i * PAIR, j * PAIR
-    store(slice(top, top + TILE), slice(left, left + TILE), real)
-    store(slice(top, top + TILE), slice(left + TILE, left + PAIR), -imag)
-    store(slice(top + TILE, top + PAIR), slice(left, left + TILE), imag)
-    store(slice(top + TILE, top + PAIR), slice(left + TILE, left + PAIR), real)
-
-
 def spread_kernel(pairs, size, where_ref, *refs):
     *parts, high_ref, low_ref, whole = refs
     half = size // 2
@@ -320,17 +325,22 @@
             start = piece_start((where_ref[0] % size) ^ (2 * n + core), size, whole.shape[0])
             whole[pl.ds(pl.multiple_of(start, 8), piece), :] = part[n * piece : (n + 1) * piece, :]
 
-    def store(rows, columns, value):
-        high, low = split(value)
-        high_ref[rows, columns] = high
-        low_ref[rows, columns] = low
+    order = high_ref.shape[0]
+
+    def store(i, j, real, imag):
+        for part, value in enumerate((real, imag)):
+            rows = slice(i * TILE, (i + 1) * TILE)
+            columns = slice(part * order + j * TILE, part * order + (j + 1) * TILE)
+            high, low = split(value)
+            high_ref[rows, columns] = high
+            low_ref[rows, columns] = low
 
     for index, (a, b) in enumerate(pairs):
         real = whole[2 * index * TILE : (2 * index + 1) * TILE, :]
         imag = whole[(2 * index + 1) * TILE : (2 * index + 2) * TILE, :]
-        embed(store, a, b, real, imag)
+        store(a, b, real, imag)
         if a != b:
-            embed(store, b, a, real.T, -imag.T)
+            store(b, a, real.T, -imag.T)
 
 
 def spread(where, parts, pairs, order):
@@ -342,10 +352,10 @@
             num_scalar_prefetch=1,
             grid=(1,),
             in_specs=[whole(part.shape) for part in parts],
-            out_specs=[whole((order, order))] * 2,
+            out_specs=[whole((order, 2 * order))] * 2,
             scratch_shapes=[pltpu.VMEM((2 * len(pairs) * TILE, TILE), F32)],
         ),
-        out_shape=[jax.ShapeDtypeStruct((order, order), BF16)] * 2,
+        out_shape=[jax.ShapeDtypeStruct((order, 2 * order), BF16)] * 2,
         name="spread",
         cost_estimate=cost(3),
     )(where, *parts)
@@ -486,36 +496,40 @@
                 matrix[rows(i), cols(k, 1)] = nothing
                 matrix[rows(i), :] -= dot3(column[rows(i)], tall)
 
-    def store(at_rows, at_columns, value):
-        high, low = split(value)
-        inv_high[at_rows, at_columns] = high
-        inv_low[at_rows, at_columns] = low
-
     weights = []
+    lane = lax.broadcasted_iota(jnp.int32, (TILE, 2 * order), 1)
+    sublane = lax.broadcasted_iota(jnp.int32, (TILE, 2 * order), 0)
     for i in range(blocks):
-        for j in range(blocks):
-            real, imag = matrix[rows(i), cols(j, 0)], matrix[rows(i), cols(j, 1)]
-            if i == j:
-                weight = jnp.sum(jnp.where(diagonal, real, 0.0), axis=1, keepdims=True)
-                weights += [weight, weight]
-                real = jnp.where(diagonal, 0.0, real)
-            embed(store, i, j, real, imag)
+        on_diagonal = lane == sublane + i * TILE
+        found = matrix[rows(i), :]
+        weights.append(jnp.sum(jnp.where(on_diagonal, found, 0.0), axis=1, keepdims=True))
+        inv_high[rows(i), :], inv_low[rows(i), :] = split(jnp.where(on_diagonal, 0.0, found))
     for copy in copies[2:]:
         copy.wait()
-    vectors = steering_ref[...].reshape(2 * order, owned)
+
+    def turn(pair):
+        return jnp.concatenate([pair, jnp.concatenate([-pair[:, owned:], pair[:, :owned]], axis=1)], axis=0)
+
+    def over_channels(pair):
+        total = jnp.sum(pair, axis=0, keepdims=True)
+        return total[:, :owned] + total[:, owned:]
+
+    vectors = jnp.concatenate(
+        [jnp.concatenate([steering_ref[b, :TILE, :], steering_ref[b, TILE:, :]], axis=1) for b in range(blocks)], axis=0
+    )
     wide = vectors.astype(F32)
-    solved = dot(inv_high[...], vectors) + dot(inv_low[...], vectors) + jnp.concatenate(weights, axis=0) * wide
-    norms = jnp.sum(solved * wide, axis=0, keepdims=True)
-    near = solved.astype(BF16)
-    turned = dot(high_ref[...], near) + dot(low_ref[...], near)
-    energy = jnp.sum(turned * solved, axis=0, keepdims=True)
-    out_ref[...] = energy / (shots * norms * norms)
+    right = turn(vectors)
+    solved = dot(inv_high[...], right) + dot(inv_low[...], right) + jnp.concatenate(weights, axis=0) * wide
+    norms = over_channels(solved * wide)
+    right = turn(solved.astype(BF16))
+    turned = dot(high_ref[...], right) + dot(low_ref[...], right)
+    out_ref[...] = over_channels(turned * solved) / (shots * norms * norms)
 
 
 def next_powers(where, mine, other, steering, sample, owned, pairs, shots):
     blocks = steering.shape[1]
     order = blocks * TILE
-    square = pltpu.VMEM((2 * order, 2 * order), BF16)
+    half = pltpu.VMEM((order, 2 * order), BF16)
     operands = (mine, other, steering, *sample)
     grid_spec = pltpu.PrefetchScalarGridSpec(
         num_scalar_prefetch=1,
@@ -526,12 +540,12 @@
             pltpu.VMEM(mine.shape, F32),
             pltpu.VMEM(other.shape, F32),
             pltpu.VMEM((blocks, PAIR, owned), BF16),
-            square,
-            square,
+            half,
+            half,
             pltpu.VMEM((order, 2 * order), F32),
             pltpu.VMEM((TILE, PAIR), F32),
-            square,
-            square,
+            half,
+            half,
             pltpu.SemaphoreType.DMA((len(operands),)),
         ],
     )
@@ -565,8 +579,8 @@
     width = max(owned, WIDTH)
     tables = angle_tables(phases, jitter, width // GV)
     every = [(a, b) for a in range(channels // TILE) for b in range(a + 1)]
-    gram, rows = sample_terms(cube, select - snap_index * cube.shape[2], every)
-    piece = halve(gram.reshape(-1, TILE), "snap", 0)
+    keep, give, rows = sample_terms(where, cube, select - snap_index * cube.shape[2], every)
+    piece = (keep + swap(give, "snap", 1)).reshape(-1, TILE)
     for bit in range(1, snap_count.bit_length() - 1):
         piece = halve(piece, "snap", bit)
     steering, energy = fill_steering(where, tables, channels // TILE, owned, width, 0, shots=rows)
@@ -587,7 +601,7 @@
     for m in range(2, snap_count, 2):
         others.append(swap(piece, "snap", m))
     both = jnp.concatenate([piece] + others, axis=0)
-    sample = spread(where, [both, swap(both, "snap", 1)], every, 2 * channels)
+    sample = spread(where, [both, swap(both, "snap", 1)], every, channels)
     powers = iteration(gathered)
     return lax.fori_loop(1, ITERS, lambda _, powers: iteration(gather_relative(powers)), powers)[0]
 

time: 270 us -> 267 us (0.989)
  transfers between devices with their start and end apart: 35 -> 35, of which waited for: 19 -> 19; matrix products, arithmetic and copies ran while one was open for 2% -> 2% of each run, Pallas kernels for 20% -> 19%
where the time goes in v2:
time: 267 us; the launch traced here: 266 us
  Pallas kernels  179 us (67%)
  starting transfers between devices  37.7 us (14%)
  waiting for transfers between devices  35.9 us (13%)
  local copies, waits for them, and re-layouts  6.39 us (2%)
  other arithmetic  5.97 us (2%)
    pallas_call x3, Pallas kernels, next_powers(): pl.pallas_call(functools.partial(step_kernel, pairs, shots), grid_spec=gr...  85.3 us
    pallas_call x3, Pallas kernels, covariance_half(): pl.pallas_call(functools.partial(covariance_kernel, slots), grid_spec=gri...  56.2 us
    ppermute x35, starting transfers between devices, swap(): return lax.ppermute(x, axis, [(i, i ^ mask) for i in range(size)])  37.7 us
    ppermute x35, waiting for transfers between devices, swap(): return lax.ppermute(x, axis, [(i, i ^ mask) for i in range(size)])  35.9 us
    pallas_call x4, Pallas kernels, fill_steering(): pl.pallas_call(functools.partial(kernel, chunk_of), grid_spec=pltpu.Prefe...  29.7 us
  transfers between devices with their start and end apart: 35, of which 19 were waited for; matrix products, arithmetic and copies ran while one was open for 2% of the time, Pallas kernels for 19%

profile of v2, /device:TPU:0, one launch (start us, length us, event | category | flops | bytes accessed | tf_op | source)
XLA Modules:
  0.0 265.6 jit_solution(3237756404422275330)
XLA Ops:
  1.3 4.5 %sample.1 = (f32[10,128,128]{2,1,0:T(8,128)}, f32[10,128,128]{2,1,0:T(8,128)}, bf16[256,1024]{1,0:T(8,128)(2,1)}) custom-call(s32[2]{0:T(128)S(1)} %pad_add_fusion.where_ref, bf16[2,512,1024]{2,1,0:T(8,128)(2,1)} %cube_ref.1, s32[1,128]{1,0:T(1,128)} %subtract_bitcast_fusion.select_ref), custom_call_target="tpu_custom_call" | custom-call | flops 4000000000 | bytes 12000000 | tf_op jit(solution)/shard_map/sample/pallas_call | solution.py:197
  8.2 2.7 %fusion = (f32[2,512,128]{2,1,0:T(8,128)}, f32[2,512,128]{2,1,0:T(8,128)}) fusion(f32[1,512,128]{2,1,0:T(8,128)S(1)} %multiply_add_fusion, f32[1,512,128]{2,1,0:T(8,128)S(1)} %multiply_multiply_fusion), kind=kLoop, calls=%fused_computation.2 | loop fusion | flops 131072 | bytes 1572864 | tf_op jit(solution)/shard_map/sin | solution.py:85
  10.9 9.7 %near_steering.1 = (bf16[8,4,256,2048]{3,2,1,0:T(8,128)(2,1)}, f32[2,1,2048]{2,1,0:T(1,128)}) custom-call(s32[2]{0:T(128)S(1)} %pad_add_fusion.where_ref, f32[2,512,128]{2,1,0:T(8,128)} %get-tuple-element.82.real_ref, f32[2,512,128]{2,1,0:T(8,128)} %get-tuple-element.81.imag_ref, bf16[256,1024]{1,0:T(8,128)(2,1)} %get-tuple-element.54.shots_ref), custom_call_target="tpu_custom_call" | custom-call | flops 8000000000 | bytes 24000000 | tf_op jit(solution)/shard_map/near_steering/pallas_call | solution.py:152
  21.6 6.6 %far_steering.3.before_ref = bf16[8,4,256,2048]{3,2,1,0:T(8,128)(2,1)} custom-call(s32[2]{0:T(128)S(1)} %pad_add_fusion.where_ref, f32[2,512,128]{2,1,0:T(8,128)} %get-tuple-element.82.real_ref, f32[2,512,128]{2,1,0:T(8,128)} %get-tuple-element.81.imag_ref, bf16[8,4,256,2048]{3,2,1,0:T(8,128)(2,1)} %get-tuple-element.55.before_ref), custom_call_target="tpu_custom_call", output_to_operand_aliasing={{}: (3, {})} | custom-call | flops 5000000000 | bytes 15000000 | tf_op jit(solution)/shard_map/far_steering/pallas_call | solution.py:152
  28.2 3.1 %collective-permute-start.9 = (f32[1,512]{1,0:T(1,128)S(1)}, f32[1,512]{1,0:T(1,128)S(1)}, u32[]{:S(2)}, u32[]{:S(2)}) collective-permute-start(f32[1,512]{1,0:T(1,128)S(1)} %get-tuple-element.85), channel_id=1, source_target_pairs={{0,2},{1,3},{2,0},{3,1},{4,6},{5,7},{6,4},{7,5},{8,10},{9,11},{10,... | collective-permute-start | bytes 6152 | tf_op jit(solution)/shard_map/ppermute | solution.py:218
  31.3 2.5 collective-permute-start.11
  33.9 6.6 %far_steering.4.before_ref = bf16[8,4,256,2048]{3,2,1,0:T(8,128)(2,1)} custom-call(s32[2]{0:T(128)S(1)} %pad_add_fusion.where_ref, f32[2,512,128]{2,1,0:T(8,128)} %get-tuple-element.82.real_ref, f32[2,512,128]{2,1,0:T(8,128)} %get-tuple-element.81.imag_ref, bf16[8,4,256,2048]{3,2,1,0:T(8,128)(2,1)} %far_steering.3.before_ref), custom_call_target="tpu_custom_call", output_to_operand_aliasing={{}: (3, {})} | custom-call | flops 5000000000 | bytes 15000000 | tf_op jit(solution)/shard_map/far_steering/pallas_call | solution.py:152
  40.9 1.9 collective-permute-start.20
  42.7 6.7 %far_steering.5.steering_ref.steering_any = bf16[8,4,256,2048]{3,2,1,0:T(8,128)(2,1)} custom-call(s32[2]{0:T(128)S(1)} %pad_add_fusion.where_ref, f32[2,512,128]{2,1,0:T(8,128)} %get-tuple-element.82.real_ref, f32[2,512,128]{2,1,0:T(8,128)} %get-tuple-element.81.imag_ref, ...), custom_call_target="tpu_custom_call", output_to_operand_aliasing={{}: (3, {})} | custom-call | flops 5000000000 | bytes 15000000 | tf_op jit(solution)/shard_map/far_steering/pallas_call | solution.py:152
  49.4 2.5 collective-permute-start.15
  51.9 1.9 collective-permute-start.13
  56.5 2.4 collective-permute-start.18
  60.0 3.7 %collective-permute-done.21 = f32[320,128]{1,0:T(8,128)S(1)} collective-permute-done((f32[320,128]{1,0:T(8,128)S(1)}, f32[320,128]{1,0:T(8,128)S(1)}, u32[]{:S(2)}, u32[]{:S(2)}) %collective-permute-start.21) | collective-permute-done | bytes 163872 | tf_op jit(solution)/shard_map/ppermute | solution.py:218
  64.3 2.5 collective-permute-start.25
  67.4 3.0 %collective-permute-done.23 = f32[320,128]{1,0:T(8,128)S(1)} collective-permute-done((f32[320,128]{1,0:T(8,128)S(1)}, f32[320,128]{1,0:T(8,128)S(1)}, u32[]{:S(2)}, u32[]{:S(2)}) %collective-permute-start.23) | collective-permute-done | bytes 163872 | tf_op jit(solution)/shard_map/ppermute | solution.py:218
  70.4 11.3 %collective-permute-done.24 = f32[320,128]{1,0:T(8,128)S(1)} collective-permute-done((f32[320,128]{1,0:T(8,128)S(1)}, f32[320,128]{1,0:T(8,128)S(1)}, u32[]{:S(2)}, u32[]{:S(2)}) %collective-permute-start.24) | collective-permute-done | bytes 163872 | tf_op jit(solution)/shard_map/ppermute | solution.py:218
  81.9 18.7 %covariance.2.mine_any = f32[10,128,128]{2,1,0:T(8,128)} custom-call(s32[8]{0:T(128)S(1)} %pad_add_fusion.1.table_ref, bf16[8,4,256,2048]{3,2,1,0:T(8,128)(2,1)} %far_steering.5.steering_ref.steering_any, f32[8,512]{1,0:T(8,128)} %copy-done.4, f32[8,512]{1,0:T(8,128)} %copy-done.12, f32[8,512]{1,0:T(8,128)} %copy-done.11, f32[8,512]{1,0:T(8,128)} %copy-done.10), custom_call_target="tpu_custom_call" | custom-call | flops 16999999488 | bytes 51000000 | tf_op jit(solution)/shard_map/covariance/pallas_call | solution.py:310
  102.0 3.3 %spread.1 = (bf16[512,1024]{1,0:T(8,128)(2,1)S(1)}, bf16[512,1024]{1,0:T(8,128)(2,1)}) custom-call(s32[2]{0:T(128)S(1)} %pad_add_fusion.where_ref, f32[1280,128]{1,0:T(8,128)} %copy-done.3, f32[1280,128]{1,0:T(8,128)} %copy-done.7), custom_call_target="tpu_custom_call" | custom-call | flops 3000000000 | bytes 9000000 | tf_op jit(solution)/shard_map/spread/pallas_call | solution.py:349
  106.2 28.5 %step.2 = f32[1,512]{1,0:T(1,128)S(1)} custom-call(s32[2]{0:T(128)S(1)} %pad_add_fusion.where_ref, f32[10,128,128]{2,1,0:T(8,128)} %covariance.2.mine_any, f32[10,128,128]{2,1,0:T(8,128)} %copy-done.8, bf16[8,4,256,2048]{3,2,1,0:T(8,128)(2,1)} %far_steering.5.steering_ref.steering_any, bf16[512,1024]{1,0:T(8,128)(2,1)S(1)} %get-tuple-element.140.high_any, ...), custom_call_target="tpu_custom_call" | custom-call | flops 28000000000 | bytes 84000000 | tf_op jit(solution)/shard_map/step/pallas_call | solution.py:552
  134.7 130.3 %while.10 = (s32[]{:T(128)}, f32[1,512]{1,0:T(1,128)S(1)}, s32[8]{0:T(128)S(1)}, bf16[8,4,256,2048]{3,2,1,0:T(8,128)(2,1)}, s32[2]{0:T(128)S(1)}, /*index=5*/bf1...) while((s32[]{:T(128)}, f32[1,512]{1,0:T(1,128)S(1)}, s32[8]{0:T(128)S(1)}, ...), condition=%wide.region_1.2_spmd, body=%wide.region_0.1_spmd.sunk | while | flops 44999999488 | bytes 140800496 | solution.py:606
  136.2 2.5 collective-permute-start.3
  138.7 2.0 collective-permute-start.1
  143.2 2.4 collective-permute-start.6
  150.5 18.7 %covariance.3.mine_any = f32[10,128,128]{2,1,0:T(8,128)} custom-call(s32[8]{0:T(128)S(1)} %get-tuple-element.153.table_ref, bf16[8,4,256,2048]{3,2,1,0:T(8,128)(2,1)} %get-tuple-element.154.steering_ref.steering_any, f32[8,512]{1,0:T(8,128)} %copy-done.1, f32[8,512]{1,0:T(8,128)} %copy-done.15, f32[8,512]{1,0:T(8,128)} %copy-done.14, f32[8,512]{1,0:T(8,128)} %copy-done.13), custom_call_target="tpu_custom_call" | custom-call | flops 16999999488 | bytes 51000000 | tf_op jit(solution)/shard_map/while/body/eval_jaxpr/covariance/pallas_call | solution.py:310
  169.2 2.3 collective-permute-done.7.other_any
  172.4 28.4 %step.3 = f32[1,512]{1,0:T(1,128)S(1)} custom-call(s32[2]{0:T(128)S(1)} %get-tuple-element.155.where_ref, f32[10,128,128]{2,1,0:T(8,128)} %covariance.3.mine_any, f32[10,128,128]{2,1,0:T(8,128)} %copy-done.9, bf16[8,4,256,2048]{3,2,1,0:T(8,128)(2,1)} %get-tuple-element.154.steering_ref.steering_any, bf16[512,1024]{1,0:T(8,128)(2,1)S(1)} %get-tuple-element.156.high_any, ...), custom_call_target="tpu_custom_call" | custom-call | flops 28000000000 | bytes 84000000 | tf_op jit(solution)/shard_map/while/body/eval_jaxpr/step/pallas_call | solution.py:552
  202.0 1.5 collective-permute-start.3
  204.6 1.8 collective-permute-start.1
  208.3 1.6 collective-permute-start.6
  214.8 18.8 %covariance.3.mine_any = f32[10,128,128]{2,1,0:T(8,128)} custom-call(s32[8]{0:T(128)S(1)} %get-tuple-element.153.table_ref, bf16[8,4,256,2048]{3,2,1,0:T(8,128)(2,1)} %get-tuple-element.154.steering_ref.steering_any, f32[8,512]{1,0:T(8,128)} %copy-done.1, f32[8,512]{1,0:T(8,128)} %copy-done.15, f32[8,512]{1,0:T(8,128)} %copy-done.14, f32[8,512]{1,0:T(8,128)} %copy-done.13), custom_call_target="tpu_custom_call" | custom-call | flops 16999999488 | bytes 51000000 | tf_op jit(solution)/shard_map/while/body/eval_jaxpr/covariance/pallas_call | solution.py:310
  233.5 2.3 collective-permute-done.7.other_any
  236.7 28.4 %step.3 = f32[1,512]{1,0:T(1,128)S(1)} custom-call(s32[2]{0:T(128)S(1)} %get-tuple-element.155.where_ref, f32[10,128,128]{2,1,0:T(8,128)} %covariance.3.mine_any, f32[10,128,128]{2,1,0:T(8,128)} %copy-done.9, bf16[8,4,256,2048]{3,2,1,0:T(8,128)(2,1)} %get-tuple-element.154.steering_ref.steering_any, bf16[512,1024]{1,0:T(8,128)(2,1)S(1)} %get-tuple-element.156.high_any, ...), custom_call_target="tpu_custom_call" | custom-call | flops 28000000000 | bytes 84000000 | tf_op jit(solution)/shard_map/while/body/eval_jaxpr/step/pallas_call | solution.py:552
  (131 shorter events, 32.0 us)
Async XLA Ops:
  5.8 34.9 %collective-permute-start.19 = (f32[10,128,128]{2,1,0:T(8,128)}, f32[10,128,128]{2,1,0:T(8,128)S(1)}, u32[]{:S(2)}, u32[]{:S(2)}) collective-permute-start(f32[10,128,128]{2,1,0:T(8,128)} %get-tuple-element.58), channel_id=1, source_target_pairs={{0,1},{1,0},{2,3},{3,2},{4,5},{5,4},{6,7},{7,6},{8,9},{9,8},{10,11... | collective-permute-start | bytes 1966088 | tf_op jit(solution)/shard_map/ppermute | solution.py:218
  21.5 6.7 %collective-permute-start.8 = (f32[4,512]{1,0:T(4,128)S(1)}, f32[4,512]{1,0:T(4,128)S(1)}, u32[]{:S(2)}, u32[]{:S(2)}) collective-permute-start(f32[4,512]{1,0:T(4,128)S(1)} %bitcast.17), channel_id=1, source_target_pairs={{0,1},{1,0},{2,3},{3,2},{4,5},{5,4},{6,7},{7,6},{8,9},{9,8},{10,11... | collective-permute-start | bytes 24584 | tf_op jit(solution)/shard_map/ppermute | solution.py:218
  28.2 12.4 %collective-permute-start.9 = (f32[1,512]{1,0:T(1,128)S(1)}, f32[1,512]{1,0:T(1,128)S(1)}, u32[]{:S(2)}, u32[]{:S(2)}) collective-permute-start(f32[1,512]{1,0:T(1,128)S(1)} %get-tuple-element.85), channel_id=1, source_target_pairs={{0,2},{1,3},{2,0},{3,1},{4,6},{5,7},{6,4},{7,5},{8,10},{9,11},{10,... | collective-permute-start | bytes 6152 | tf_op jit(solution)/shard_map/ppermute | solution.py:218
  31.3 9.2 %collective-permute-start.11 = (f32[1,512]{1,0:T(1,128)S(1)}, f32[1,512]{1,0:T(1,128)S(1)}, u32[]{:S(2)}, u32[]{:S(2)}) collective-permute-start(f32[1,512]{1,0:T(1,128)S(1)} %get-tuple-element.86), channel_id=1, source_target_pairs={{0,6},{1,7},{2,4},{3,5},{4,2},{5,3},{6,0},{7,1},{8,14},{9,15},{10,... | collective-permute-start | bytes 6152 | tf_op jit(solution)/shard_map/ppermute | solution.py:218
  33.8 6.8 %collective-permute-start.10 = (f32[1,512]{1,0:T(1,128)S(1)}, f32[1,512]{1,0:T(1,128)S(1)}, u32[]{:S(2)}, u32[]{:S(2)}) collective-permute-start(f32[1,512]{1,0:T(1,128)S(1)} %get-tuple-element.87), channel_id=1, source_target_pairs={{0,4},{1,5},{2,6},{3,7},{4,0},{5,1},{6,2},{7,3},{8,12},{9,13},{10,... | collective-permute-start | bytes 6152 | tf_op jit(solution)/shard_map/ppermute | solution.py:218
  40.6 8.8 %collective-permute-start.12 = (f32[1,512]{1,0:T(1,128)S(1)}, f32[1,512]{1,0:T(1,128)S(1)}, u32[]{:S(2)}, u32[]{:S(2)}) collective-permute-start(f32[1,512]{1,0:T(1,128)S(1)} %fusion.15), channel_id=1, source_target_pairs={{0,1},{1,0},{2,3},{3,2},{4,5},{5,4},{6,7},{7,6},{8,9},{9,8},{10,11... | collective-permute-start | bytes 6152 | tf_op jit(solution)/shard_map/ppermute | solution.py:218
  40.9 13.0 %collective-permute-start.20 = (f32[640,128]{1,0:T(8,128)S(1)}, f32[640,128]{1,0:T(8,128)S(1)}, u32[]{:S(2)}, u32[]{:S(2)}) collective-permute-start(f32[640,128]{1,0:T(8,128)S(1)} %constant_dynamic-slice_fusion.1), channel_id=1, source_target_pairs={{0,2},{1,3},{2,0},{3,1},{4,6},{5,7},{6,4},{7,5},{8,10},{9,11},{10,... | collective-permute-start | bytes 983048 | tf_op jit(solution)/shard_map/ppermute | solution.py:218
  49.4 5.6 %collective-permute-start.15 = (f32[2,512]{1,0:T(2,128)S(1)}, f32[2,512]{1,0:T(2,128)S(1)}, u32[]{:S(2)}, u32[]{:S(2)}) collective-permute-start(f32[2,512]{1,0:T(2,128)S(1)} %pad_maximum_fusion.2), channel_id=1, source_target_pairs={{0,6},{1,7},{2,4},{3,5},{4,2},{5,3},{6,0},{7,1},{8,14},{9,15},{10,... | collective-permute-start | bytes 12296 | tf_op jit(solution)/shard_map/ppermute | solution.py:218
  51.9 4.5 %collective-permute-start.14 = (f32[2,512]{1,0:T(2,128)S(1)}, f32[2,512]{1,0:T(2,128)S(1)}, u32[]{:S(2)}, u32[]{:S(2)}) collective-permute-start(f32[2,512]{1,0:T(2,128)S(1)} %pad_maximum_fusion.2), channel_id=1, source_target_pairs={{0,4},{1,5},{2,6},{3,7},{4,0},{5,1},{6,2},{7,3},{8,12},{9,13},{10,... | collective-permute-start | bytes 12296 | tf_op jit(solution)/shard_map/ppermute | solution.py:218
  51.9 4.5 %collective-permute-start.13 = (f32[2,512]{1,0:T(2,128)S(1)}, f32[2,512]{1,0:T(2,128)S(1)}, u32[]{:S(2)}, u32[]{:S(2)}) collective-permute-start(f32[2,512]{1,0:T(2,128)S(1)} %pad_maximum_fusion.2), channel_id=1, source_target_pairs={{0,2},{1,3},{2,0},{3,1},{4,6},{5,7},{6,4},{7,5},{8,10},{9,11},{10,... | collective-permute-start | bytes 12296 | tf_op jit(solution)/shard_map/ppermute | solution.py:218
  53.9 9.8 %collective-permute-start.21 = (f32[320,128]{1,0:T(8,128)S(1)}, f32[320,128]{1,0:T(8,128)S(1)}, u32[]{:S(2)}, u32[]{:S(2)}) collective-permute-start(f32[320,128]{1,0:T(8,128)S(1)} %constant_dynamic-slice_fusion), channel_id=1, source_target_pairs={{0,4},{1,5},{2,6},{3,7},{4,0},{5,1},{6,2},{7,3},{8,12},{9,13},{10,... | collective-permute-start | bytes 491528 | tf_op jit(solution)/shard_map/ppermute | solution.py:218
  56.5 7.2 %collective-permute-start.18 = (f32[8,512]{1,0:T(8,128)S(1)}, f32[8,512]{1,0:T(8,128)S(1)}, u32[]{:S(2)}, u32[]{:S(2)}) collective-permute-start(f32[8,512]{1,0:T(8,128)S(1)} %concatenate.22.refs_0_), channel_id=1, source_target_pairs={{0,24},{8,16},{16,8},{24,0},{1,25},{9,17},{17,9},{25,1},{2,26},{10... | collective-permute-start | bytes 49160 | tf_op jit(solution)/shard_map/ppermute | solution.py:218
  58.9 4.8 %collective-permute-start.17 = (f32[8,512]{1,0:T(8,128)S(1)}, f32[8,512]{1,0:T(8,128)S(1)}, u32[]{:S(2)}, u32[]{:S(2)}) collective-permute-start(f32[8,512]{1,0:T(8,128)S(1)} %concatenate.22.refs_0_), channel_id=1, source_target_pairs={{0,16},{8,24},{16,0},{24,8},{1,17},{9,25},{17,1},{25,9},{2,18},{10... | collective-permute-start | bytes 49160 | tf_op jit(solution)/shard_map/ppermute | solution.py:218
  59.4 4.3 %collective-permute-start.16 = (f32[8,512]{1,0:T(8,128)S(1)}, f32[8,512]{1,0:T(8,128)S(1)}, u32[]{:S(2)}, u32[]{:S(2)}) collective-permute-start(f32[8,512]{1,0:T(8,128)S(1)} %concatenate.22.refs_0_), channel_id=1, source_target_pairs={{0,8},{8,0},{16,24},{24,16},{1,9},{9,1},{17,25},{25,17},{2,10},{10... | collective-permute-start | bytes 49160 | tf_op jit(solution)/shard_map/ppermute | solution.py:218
  63.8 6.6 %collective-permute-start.23 = (f32[320,128]{1,0:T(8,128)S(1)}, f32[320,128]{1,0:T(8,128)S(1)}, u32[]{:S(2)}, u32[]{:S(2)}) collective-permute-start(f32[320,128]{1,0:T(8,128)S(1)} %dynamic-slice_add_fusion.1), channel_id=1, source_target_pairs={{0,2},{1,3},{2,0},{3,1},{4,6},{5,7},{6,4},{7,5},{8,10},{9,11},{10,... | collective-permute-start | bytes 491528 | tf_op jit(solution)/shard_map/ppermute | solution.py:218
  64.3 17.5 %collective-permute-start.25 = (f32[320,128]{1,0:T(8,128)S(1)}, f32[320,128]{1,0:T(8,128)S(1)}, u32[]{:S(2)}, u32[]{:S(2)}) collective-permute-start(f32[320,128]{1,0:T(8,128)S(1)} %dynamic-slice_add_fusion.1), channel_id=1, source_target_pairs={{0,6},{1,7},{2,4},{3,5},{4,2},{5,3},{6,0},{7,1},{8,14},{9,15},{10,... | collective-permute-start | bytes 491528 | tf_op jit(solution)/shard_map/ppermute | solution.py:218
  66.8 15.0 %collective-permute-start.24 = (f32[320,128]{1,0:T(8,128)S(1)}, f32[320,128]{1,0:T(8,128)S(1)}, u32[]{:S(2)}, u32[]{:S(2)}) collective-permute-start(f32[320,128]{1,0:T(8,128)S(1)} %dynamic-slice_add_fusion.1), channel_id=1, source_target_pairs={{0,4},{1,5},{2,6},{3,7},{4,0},{5,1},{6,2},{7,3},{8,12},{9,13},{10,... | collective-permute-start | bytes 491528 | tf_op jit(solution)/shard_map/ppermute | solution.py:218
  81.8 19.3 %collective-permute-start.26 = (f32[1280,128]{1,0:T(8,128)S(1)}, f32[1280,128]{1,0:T(8,128)S(1)}, u32[]{:S(2)}, u32[]{:S(2)}) collective-permute-start(f32[1280,128]{1,0:T(8,128)S(1)} %constant_dynamic-update-slice_fusion.refs_0_), channel_id=1, source_target_pairs={{0,1},{1,0},{2,3},{3,2},{4,5},{5,4},{6,7},{7,6},{8,9},{9,8},{10,11... | collective-permute-start | bytes 1966088 | tf_op jit(solution)/shard_map/ppermute | solution.py:218
  100.7 4.7 %collective-permute-start.22 = (f32[10,128,128]{2,1,0:T(8,128)}, f32[10,128,128]{2,1,0:T(8,128)S(1)}, u32[]{:S(2)}, u32[]{:S(2)}) collective-permute-start(f32[10,128,128]{2,1,0:T(8,128)} %covariance.2.mine_any), channel_id=1, source_target_pairs={{0,1},{1,0},{2,3},{3,2},{4,5},{5,4},{6,7},{7,6},{8,9},{9,8},{10,11... | collective-permute-start | bytes 1966088 | tf_op jit(solution)/shard_map/ppermute | solution.py:218
  136.2 5.5 %collective-permute-start.3 = (f32[2,512]{1,0:T(2,128)S(1)}, f32[2,512]{1,0:T(2,128)S(1)}, u32[]{:S(2)}, u32[]{:S(2)}) collective-permute-start(f32[2,512]{1,0:T(2,128)S(1)} %pad_maximum_fusion.4), channel_id=1, source_target_pairs={{0,6},{1,7},{2,4},{3,5},{4,2},{5,3},{6,0},{7,1},{8,14},{9,15},{10,... | collective-permute-start | bytes 12296 | tf_op jit(solution)/shard_map/while/body/eval_jaxpr/ppermute | solution.py:218
  138.7 4.5 %collective-permute-start.2 = (f32[2,512]{1,0:T(2,128)S(1)}, f32[2,512]{1,0:T(2,128)S(1)}, u32[]{:S(2)}, u32[]{:S(2)}) collective-permute-start(f32[2,512]{1,0:T(2,128)S(1)} %pad_maximum_fusion.4), channel_id=1, source_target_pairs={{0,4},{1,5},{2,6},{3,7},{4,0},{5,1},{6,2},{7,3},{8,12},{9,13},{10,... | collective-permute-start | bytes 12296 | tf_op jit(solution)/shard_map/while/body/eval_jaxpr/ppermute | solution.py:218
  138.7 4.5 %collective-permute-start.1 = (f32[2,512]{1,0:T(2,128)S(1)}, f32[2,512]{1,0:T(2,128)S(1)}, u32[]{:S(2)}, u32[]{:S(2)}) collective-permute-start(f32[2,512]{1,0:T(2,128)S(1)} %pad_maximum_fusion.4), channel_id=1, source_target_pairs={{0,2},{1,3},{2,0},{3,1},{4,6},{5,7},{6,4},{7,5},{8,10},{9,11},{10,... | collective-permute-start | bytes 12296 | tf_op jit(solution)/shard_map/while/body/eval_jaxpr/ppermute | solution.py:218
  143.2 4.8 %collective-permute-start.6 = (f32[8,512]{1,0:T(8,128)S(1)}, f32[8,512]{1,0:T(8,128)S(1)}, u32[]{:S(2)}, u32[]{:S(2)}) collective-permute-start(f32[8,512]{1,0:T(8,128)S(1)} %concatenate.25.refs_0_), channel_id=1, source_target_pairs={{0,24},{8,16},{16,8},{24,0},{1,25},{9,17},{17,9},{25,1},{2,26},{10... | collective-permute-start | bytes 49160 | tf_op jit(solution)/shard_map/while/body/eval_jaxpr/ppermute | solution.py:218
  145.6 3.7 %collective-permute-start.5 = (f32[8,512]{1,0:T(8,128)S(1)}, f32[8,512]{1,0:T(8,128)S(1)}, u32[]{:S(2)}, u32[]{:S(2)}) collective-permute-start(f32[8,512]{1,0:T(8,128)S(1)} %concatenate.25.refs_0_), channel_id=1, source_target_pairs={{0,16},{8,24},{16,0},{24,8},{1,17},{9,25},{17,1},{25,9},{2,18},{10... | collective-permute-start | bytes 49160 | tf_op jit(solution)/shard_map/while/body/eval_jaxpr/ppermute | solution.py:218
  146.2 3.7 %collective-permute-start.4 = (f32[8,512]{1,0:T(8,128)S(1)}, f32[8,512]{1,0:T(8,128)S(1)}, u32[]{:S(2)}, u32[]{:S(2)}) collective-permute-start(f32[8,512]{1,0:T(8,128)S(1)} %concatenate.25.refs_0_), channel_id=1, source_target_pairs={{0,8},{8,0},{16,24},{24,16},{1,9},{9,1},{17,25},{25,17},{2,10},{10... | collective-permute-start | bytes 49160 | tf_op jit(solution)/shard_map/while/body/eval_jaxpr/ppermute | solution.py:218
  169.2 2.3 collective-permute-start.7
  202.0 5.5 %collective-permute-start.3 = (f32[2,512]{1,0:T(2,128)S(1)}, f32[2,512]{1,0:T(2,128)S(1)}, u32[]{:S(2)}, u32[]{:S(2)}) collective-permute-start(f32[2,512]{1,0:T(2,128)S(1)} %pad_maximum_fusion.4), channel_id=1, source_target_pairs={{0,6},{1,7},{2,4},{3,5},{4,2},{5,3},{6,0},{7,1},{8,14},{9,15},{10,... | collective-permute-start | bytes 12296 | tf_op jit(solution)/shard_map/while/body/eval_jaxpr/ppermute | solution.py:218
  203.6 4.5 %collective-permute-start.2 = (f32[2,512]{1,0:T(2,128)S(1)}, f32[2,512]{1,0:T(2,128)S(1)}, u32[]{:S(2)}, u32[]{:S(2)}) collective-permute-start(f32[2,512]{1,0:T(2,128)S(1)} %pad_maximum_fusion.4), channel_id=1, source_target_pairs={{0,4},{1,5},{2,6},{3,7},{4,0},{5,1},{6,2},{7,3},{8,12},{9,13},{10,... | collective-permute-start | bytes 12296 | tf_op jit(solution)/shard_map/while/body/eval_jaxpr/ppermute | solution.py:218
  204.6 3.6 %collective-permute-start.1 = (f32[2,512]{1,0:T(2,128)S(1)}, f32[2,512]{1,0:T(2,128)S(1)}, u32[]{:S(2)}, u32[]{:S(2)}) collective-permute-start(f32[2,512]{1,0:T(2,128)S(1)} %pad_maximum_fusion.4), channel_id=1, source_target_pairs={{0,2},{1,3},{2,0},{3,1},{4,6},{5,7},{6,4},{7,5},{8,10},{9,11},{10,... | collective-permute-start | bytes 12296 | tf_op jit(solution)/shard_map/while/body/eval_jaxpr/ppermute | solution.py:218
  208.3 4.7 %collective-permute-start.6 = (f32[8,512]{1,0:T(8,128)S(1)}, f32[8,512]{1,0:T(8,128)S(1)}, u32[]{:S(2)}, u32[]{:S(2)}) collective-permute-start(f32[8,512]{1,0:T(8,128)S(1)} %concatenate.25.refs_0_), channel_id=1, source_target_pairs={{0,24},{8,16},{16,8},{24,0},{1,25},{9,17},{17,9},{25,1},{2,26},{10... | collective-permute-start | bytes 49160 | tf_op jit(solution)/shard_map/while/body/eval_jaxpr/ppermute | solution.py:218
  209.9 3.7 %collective-permute-start.5 = (f32[8,512]{1,0:T(8,128)S(1)}, f32[8,512]{1,0:T(8,128)S(1)}, u32[]{:S(2)}, u32[]{:S(2)}) collective-permute-start(f32[8,512]{1,0:T(8,128)S(1)} %concatenate.25.refs_0_), channel_id=1, source_target_pairs={{0,16},{8,24},{16,0},{24,8},{1,17},{9,25},{17,1},{25,9},{2,18},{10... | collective-permute-start | bytes 49160 | tf_op jit(solution)/shard_map/while/body/eval_jaxpr/ppermute | solution.py:218
  210.4 3.7 %collective-permute-start.4 = (f32[8,512]{1,0:T(8,128)S(1)}, f32[8,512]{1,0:T(8,128)S(1)}, u32[]{:S(2)}, u32[]{:S(2)}) collective-permute-start(f32[8,512]{1,0:T(8,128)S(1)} %concatenate.25.refs_0_), channel_id=1, source_target_pairs={{0,8},{8,0},{16,24},{24,16},{1,9},{9,1},{17,25},{25,17},{2,10},{10... | collective-permute-start | bytes 49160 | tf_op jit(solution)/shard_map/while/body/eval_jaxpr/ppermute | solution.py:218
  (25 other events, 189.9 us)

commit v3 on v2

--- a/solution.py
+++ b/solution.py
@@ -403,15 +403,15 @@
             for j in columns:
                 columns[j] = reduce(*columns[j])
         rows = jnp.concatenate([row_real, row_imag], axis=1)
-        high, low = split(rows)
+        extra = jnp.where(lane == base + sublane, 1.0, 0.0)
+        high, low = split(jnp.concatenate([row_real + extra, row_imag], axis=1))
         turned_high = jnp.concatenate([-high[:, TILE:], high[:, :TILE]], axis=1)
         turned_low = jnp.concatenate([-low[:, TILE:], low[:, :TILE]], axis=1)
         right = [high, turned_high, high, turned_high, low, turned_low]
         right += [jnp.zeros_like(low)] * (TILE // PANEL - len(right))
         update = dot(left, jnp.concatenate(right, axis=0))
-        inside = lane_all // PANEL == step
-        tile[:, :TILE] = jnp.where(inside, 0.0, real) - update[:, :TILE]
-        tile[:, TILE:] = jnp.where(inside, 0.0, imag) - update[:, TILE:]
+        tile[:, :TILE] = real - update[:, :TILE]
+        tile[:, TILE:] = imag - update[:, TILE:]
         tile[pl.ds(base, PANEL), :] = rows
         return 0
 

time: 267 us -> 267 us (level)
  no operation moved by 1% of the time
where the time goes in v3:
time: 267 us; the launch traced here: 266 us
  Pallas kernels  179 us (67%)
  starting transfers between devices  37.7 us (14%)
  waiting for transfers between devices  35.9 us (13%)
  local copies, waits for them, and re-layouts  6.39 us (2%)
  other arithmetic  5.97 us (2%)
    pallas_call x3, Pallas kernels, next_powers(): pl.pallas_call(functools.partial(step_kernel, pairs, shots), grid_spec=gr...  85.3 us
    pallas_call x3, Pallas kernels, covariance_half(): pl.pallas_call(functools.partial(covariance_kernel, slots), grid_spec=gri...  56.2 us
    ppermute x35, starting transfers between devices, swap(): return lax.ppermute(x, axis, [(i, i ^ mask) for i in range(size)])  37.7 us
    ppermute x35, waiting for transfers between devices, swap(): return lax.ppermute(x, axis, [(i, i ^ mask) for i in range(size)])  35.9 us
    pallas_call x4, Pallas kernels, fill_steering(): pl.pallas_call(functools.partial(kernel, chunk_of), grid_spec=pltpu.Prefe...  29.7 us
  transfers between devices with their start and end apart: 35, of which 19 were waited for; matrix products, arithmetic and copies ran while one was open for 2% of the time, Pallas kernels for 19%

profile of v3, /device:TPU:0, one launch (start us, length us, event | category | flops | bytes accessed | tf_op | source)
XLA Modules:
  0.0 265.6 jit_solution(15522161581574067058)
XLA Ops:
  1.3 4.5 %sample.1 = (f32[10,128,128]{2,1,0:T(8,128)}, f32[10,128,128]{2,1,0:T(8,128)}, bf16[256,1024]{1,0:T(8,128)(2,1)}) custom-call(s32[2]{0:T(128)S(1)} %pad_add_fusion.where_ref, bf16[2,512,1024]{2,1,0:T(8,128)(2,1)} %cube_ref.1, s32[1,128]{1,0:T(1,128)} %subtract_bitcast_fusion.select_ref), custom_call_target="tpu_custom_call" | custom-call | flops 4000000000 | bytes 12000000 | tf_op jit(solution)/shard_map/sample/pallas_call | solution.py:197
  8.2 2.7 %fusion = (f32[2,512,128]{2,1,0:T(8,128)}, f32[2,512,128]{2,1,0:T(8,128)}) fusion(f32[1,512,128]{2,1,0:T(8,128)S(1)} %multiply_add_fusion, f32[1,512,128]{2,1,0:T(8,128)S(1)} %multiply_multiply_fusion), kind=kLoop, calls=%fused_computation.2 | loop fusion | flops 131072 | bytes 1572864 | tf_op jit(solution)/shard_map/sin | solution.py:85
  10.9 9.7 %near_steering.1 = (bf16[8,4,256,2048]{3,2,1,0:T(8,128)(2,1)}, f32[2,1,2048]{2,1,0:T(1,128)}) custom-call(s32[2]{0:T(128)S(1)} %pad_add_fusion.where_ref, f32[2,512,128]{2,1,0:T(8,128)} %get-tuple-element.82.real_ref, f32[2,512,128]{2,1,0:T(8,128)} %get-tuple-element.81.imag_ref, bf16[256,1024]{1,0:T(8,128)(2,1)} %get-tuple-element.54.shots_ref), custom_call_target="tpu_custom_call" | custom-call | flops 8000000000 | bytes 24000000 | tf_op jit(solution)/shard_map/near_steering/pallas_call | solution.py:152
  21.6 6.6 %far_steering.3.before_ref = bf16[8,4,256,2048]{3,2,1,0:T(8,128)(2,1)} custom-call(s32[2]{0:T(128)S(1)} %pad_add_fusion.where_ref, f32[2,512,128]{2,1,0:T(8,128)} %get-tuple-element.82.real_ref, f32[2,512,128]{2,1,0:T(8,128)} %get-tuple-element.81.imag_ref, bf16[8,4,256,2048]{3,2,1,0:T(8,128)(2,1)} %get-tuple-element.55.before_ref), custom_call_target="tpu_custom_call", output_to_operand_aliasing={{}: (3, {})} | custom-call | flops 5000000000 | bytes 15000000 | tf_op jit(solution)/shard_map/far_steering/pallas_call | solution.py:152
  28.2 3.1 %collective-permute-start.9 = (f32[1,512]{1,0:T(1,128)S(1)}, f32[1,512]{1,0:T(1,128)S(1)}, u32[]{:S(2)}, u32[]{:S(2)}) collective-permute-start(f32[1,512]{1,0:T(1,128)S(1)} %get-tuple-element.85), channel_id=1, source_target_pairs={{0,2},{1,3},{2,0},{3,1},{4,6},{5,7},{6,4},{7,5},{8,10},{9,11},{10,... | collective-permute-start | bytes 6152 | tf_op jit(solution)/shard_map/ppermute | solution.py:218
  31.3 2.5 collective-permute-start.11
  33.9 6.6 %far_steering.4.before_ref = bf16[8,4,256,2048]{3,2,1,0:T(8,128)(2,1)} custom-call(s32[2]{0:T(128)S(1)} %pad_add_fusion.where_ref, f32[2,512,128]{2,1,0:T(8,128)} %get-tuple-element.82.real_ref, f32[2,512,128]{2,1,0:T(8,128)} %get-tuple-element.81.imag_ref, bf16[8,4,256,2048]{3,2,1,0:T(8,128)(2,1)} %far_steering.3.before_ref), custom_call_target="tpu_custom_call", output_to_operand_aliasing={{}: (3, {})} | custom-call | flops 5000000000 | bytes 15000000 | tf_op jit(solution)/shard_map/far_steering/pallas_call | solution.py:152
  40.9 1.9 collective-permute-start.20
  42.7 6.7 %far_steering.5.steering_ref.steering_any = bf16[8,4,256,2048]{3,2,1,0:T(8,128)(2,1)} custom-call(s32[2]{0:T(128)S(1)} %pad_add_fusion.where_ref, f32[2,512,128]{2,1,0:T(8,128)} %get-tuple-element.82.real_ref, f32[2,512,128]{2,1,0:T(8,128)} %get-tuple-element.81.imag_ref, ...), custom_call_target="tpu_custom_call", output_to_operand_aliasing={{}: (3, {})} | custom-call | flops 5000000000 | bytes 15000000 | tf_op jit(solution)/shard_map/far_steering/pallas_call | solution.py:152
  49.4 2.5 collective-permute-start.15
  51.9 1.9 collective-permute-start.13
  56.5 2.4 collective-permute-start.18
  60.0 3.7 %collective-permute-done.21 = f32[320,128]{1,0:T(8,128)S(1)} collective-permute-done((f32[320,128]{1,0:T(8,128)S(1)}, f32[320,128]{1,0:T(8,128)S(1)}, u32[]{:S(2)}, u32[]{:S(2)}) %collective-permute-start.21) | collective-permute-done | bytes 163872 | tf_op jit(solution)/shard_map/ppermute | solution.py:218
  64.3 2.5 collective-permute-start.25
  67.4 3.0 %collective-permute-done.23 = f32[320,128]{1,0:T(8,128)S(1)} collective-permute-done((f32[320,128]{1,0:T(8,128)S(1)}, f32[320,128]{1,0:T(8,128)S(1)}, u32[]{:S(2)}, u32[]{:S(2)}) %collective-permute-start.23) | collective-permute-done | bytes 163872 | tf_op jit(solution)/shard_map/ppermute | solution.py:218
  70.4 11.3 %collective-permute-done.24 = f32[320,128]{1,0:T(8,128)S(1)} collective-permute-done((f32[320,128]{1,0:T(8,128)S(1)}, f32[320,128]{1,0:T(8,128)S(1)}, u32[]{:S(2)}, u32[]{:S(2)}) %collective-permute-start.24) | collective-permute-done | bytes 163872 | tf_op jit(solution)/shard_map/ppermute | solution.py:218
  81.9 18.7 %covariance.2.mine_any = f32[10,128,128]{2,1,0:T(8,128)} custom-call(s32[8]{0:T(128)S(1)} %pad_add_fusion.1.table_ref, bf16[8,4,256,2048]{3,2,1,0:T(8,128)(2,1)} %far_steering.5.steering_ref.steering_any, f32[8,512]{1,0:T(8,128)} %copy-done.4, f32[8,512]{1,0:T(8,128)} %copy-done.12, f32[8,512]{1,0:T(8,128)} %copy-done.11, f32[8,512]{1,0:T(8,128)} %copy-done.10), custom_call_target="tpu_custom_call" | custom-call | flops 16999999488 | bytes 51000000 | tf_op jit(solution)/shard_map/covariance/pallas_call | solution.py:310
  102.0 3.3 %spread.1 = (bf16[512,1024]{1,0:T(8,128)(2,1)S(1)}, bf16[512,1024]{1,0:T(8,128)(2,1)}) custom-call(s32[2]{0:T(128)S(1)} %pad_add_fusion.where_ref, f32[1280,128]{1,0:T(8,128)} %copy-done.3, f32[1280,128]{1,0:T(8,128)} %copy-done.7), custom_call_target="tpu_custom_call" | custom-call | flops 3000000000 | bytes 9000000 | tf_op jit(solution)/shard_map/spread/pallas_call | solution.py:349
  106.2 28.5 %step.2 = f32[1,512]{1,0:T(1,128)S(1)} custom-call(s32[2]{0:T(128)S(1)} %pad_add_fusion.where_ref, f32[10,128,128]{2,1,0:T(8,128)} %covariance.2.mine_any, f32[10,128,128]{2,1,0:T(8,128)} %copy-done.8, bf16[8,4,256,2048]{3,2,1,0:T(8,128)(2,1)} %far_steering.5.steering_ref.steering_any, bf16[512,1024]{1,0:T(8,128)(2,1)S(1)} %get-tuple-element.140.high_any, ...), custom_call_target="tpu_custom_call" | custom-call | flops 28000000000 | bytes 84000000 | tf_op jit(solution)/shard_map/step/pallas_call | solution.py:552
  134.7 130.3 %while.10 = (s32[]{:T(128)}, f32[1,512]{1,0:T(1,128)S(1)}, s32[8]{0:T(128)S(1)}, bf16[8,4,256,2048]{3,2,1,0:T(8,128)(2,1)}, s32[2]{0:T(128)S(1)}, /*index=5*/bf1...) while((s32[]{:T(128)}, f32[1,512]{1,0:T(1,128)S(1)}, s32[8]{0:T(128)S(1)}, ...), condition=%wide.region_1.2_spmd, body=%wide.region_0.1_spmd.sunk | while | flops 44999999488 | bytes 140800496 | solution.py:606
  136.2 2.5 collective-permute-start.3
  138.7 2.0 collective-permute-start.1
  143.2 2.4 collective-permute-start.6
  150.5 18.7 %covariance.3.mine_any = f32[10,128,128]{2,1,0:T(8,128)} custom-call(s32[8]{0:T(128)S(1)} %get-tuple-element.153.table_ref, bf16[8,4,256,2048]{3,2,1,0:T(8,128)(2,1)} %get-tuple-element.154.steering_ref.steering_any, f32[8,512]{1,0:T(8,128)} %copy-done.1, f32[8,512]{1,0:T(8,128)} %copy-done.15, f32[8,512]{1,0:T(8,128)} %copy-done.14, f32[8,512]{1,0:T(8,128)} %copy-done.13), custom_call_target="tpu_custom_call" | custom-call | flops 16999999488 | bytes 51000000 | tf_op jit(solution)/shard_map/while/body/eval_jaxpr/covariance/pallas_call | solution.py:310
  169.2 2.3 collective-permute-done.7.other_any
  172.4 28.4 %step.3 = f32[1,512]{1,0:T(1,128)S(1)} custom-call(s32[2]{0:T(128)S(1)} %get-tuple-element.155.where_ref, f32[10,128,128]{2,1,0:T(8,128)} %covariance.3.mine_any, f32[10,128,128]{2,1,0:T(8,128)} %copy-done.9, bf16[8,4,256,2048]{3,2,1,0:T(8,128)(2,1)} %get-tuple-element.154.steering_ref.steering_any, bf16[512,1024]{1,0:T(8,128)(2,1)S(1)} %get-tuple-element.156.high_any, ...), custom_call_target="tpu_custom_call" | custom-call | flops 28000000000 | bytes 84000000 | tf_op jit(solution)/shard_map/while/body/eval_jaxpr/step/pallas_call | solution.py:552
  202.0 1.5 collective-permute-start.3
  204.6 1.8 collective-permute-start.1
  208.3 1.6 collective-permute-start.6
  214.8 18.8 %covariance.3.mine_any = f32[10,128,128]{2,1,0:T(8,128)} custom-call(s32[8]{0:T(128)S(1)} %get-tuple-element.153.table_ref, bf16[8,4,256,2048]{3,2,1,0:T(8,128)(2,1)} %get-tuple-element.154.steering_ref.steering_any, f32[8,512]{1,0:T(8,128)} %copy-done.1, f32[8,512]{1,0:T(8,128)} %copy-done.15, f32[8,512]{1,0:T(8,128)} %copy-done.14, f32[8,512]{1,0:T(8,128)} %copy-done.13), custom_call_target="tpu_custom_call" | custom-call | flops 16999999488 | bytes 51000000 | tf_op jit(solution)/shard_map/while/body/eval_jaxpr/covariance/pallas_call | solution.py:310
  233.5 2.3 collective-permute-done.7.other_any
  236.7 28.4 %step.3 = f32[1,512]{1,0:T(1,128)S(1)} custom-call(s32[2]{0:T(128)S(1)} %get-tuple-element.155.where_ref, f32[10,128,128]{2,1,0:T(8,128)} %covariance.3.mine_any, f32[10,128,128]{2,1,0:T(8,128)} %copy-done.9, bf16[8,4,256,2048]{3,2,1,0:T(8,128)(2,1)} %get-tuple-element.154.steering_ref.steering_any, bf16[512,1024]{1,0:T(8,128)(2,1)S(1)} %get-tuple-element.156.high_any, ...), custom_call_target="tpu_custom_call" | custom-call | flops 28000000000 | bytes 84000000 | tf_op jit(solution)/shard_map/while/body/eval_jaxpr/step/pallas_call | solution.py:552
  (131 shorter events, 32.1 us)
Async XLA Ops:
  5.8 34.9 %collective-permute-start.19 = (f32[10,128,128]{2,1,0:T(8,128)}, f32[10,128,128]{2,1,0:T(8,128)S(1)}, u32[]{:S(2)}, u32[]{:S(2)}) collective-permute-start(f32[10,128,128]{2,1,0:T(8,128)} %get-tuple-element.58), channel_id=1, source_target_pairs={{0,1},{1,0},{2,3},{3,2},{4,5},{5,4},{6,7},{7,6},{8,9},{9,8},{10,11... | collective-permute-start | bytes 1966088 | tf_op jit(solution)/shard_map/ppermute | solution.py:218
  21.5 6.7 %collective-permute-start.8 = (f32[4,512]{1,0:T(4,128)S(1)}, f32[4,512]{1,0:T(4,128)S(1)}, u32[]{:S(2)}, u32[]{:S(2)}) collective-permute-start(f32[4,512]{1,0:T(4,128)S(1)} %bitcast.17), channel_id=1, source_target_pairs={{0,1},{1,0},{2,3},{3,2},{4,5},{5,4},{6,7},{7,6},{8,9},{9,8},{10,11... | collective-permute-start | bytes 24584 | tf_op jit(solution)/shard_map/ppermute | solution.py:218
  28.2 12.4 %collective-permute-start.9 = (f32[1,512]{1,0:T(1,128)S(1)}, f32[1,512]{1,0:T(1,128)S(1)}, u32[]{:S(2)}, u32[]{:S(2)}) collective-permute-start(f32[1,512]{1,0:T(1,128)S(1)} %get-tuple-element.85), channel_id=1, source_target_pairs={{0,2},{1,3},{2,0},{3,1},{4,6},{5,7},{6,4},{7,5},{8,10},{9,11},{10,... | collective-permute-start | bytes 6152 | tf_op jit(solution)/shard_map/ppermute | solution.py:218
  31.3 9.2 %collective-permute-start.11 = (f32[1,512]{1,0:T(1,128)S(1)}, f32[1,512]{1,0:T(1,128)S(1)}, u32[]{:S(2)}, u32[]{:S(2)}) collective-permute-start(f32[1,512]{1,0:T(1,128)S(1)} %get-tuple-element.86), channel_id=1, source_target_pairs={{0,6},{1,7},{2,4},{3,5},{4,2},{5,3},{6,0},{7,1},{8,14},{9,15},{10,... | collective-permute-start | bytes 6152 | tf_op jit(solution)/shard_map/ppermute | solution.py:218
  33.8 6.8 %collective-permute-start.10 = (f32[1,512]{1,0:T(1,128)S(1)}, f32[1,512]{1,0:T(1,128)S(1)}, u32[]{:S(2)}, u32[]{:S(2)}) collective-permute-start(f32[1,512]{1,0:T(1,128)S(1)} %get-tuple-element.87), channel_id=1, source_target_pairs={{0,4},{1,5},{2,6},{3,7},{4,0},{5,1},{6,2},{7,3},{8,12},{9,13},{10,... | collective-permute-start | bytes 6152 | tf_op jit(solution)/shard_map/ppermute | solution.py:218
  40.6 8.8 %collective-permute-start.12 = (f32[1,512]{1,0:T(1,128)S(1)}, f32[1,512]{1,0:T(1,128)S(1)}, u32[]{:S(2)}, u32[]{:S(2)}) collective-permute-start(f32[1,512]{1,0:T(1,128)S(1)} %fusion.15), channel_id=1, source_target_pairs={{0,1},{1,0},{2,3},{3,2},{4,5},{5,4},{6,7},{7,6},{8,9},{9,8},{10,11... | collective-permute-start | bytes 6152 | tf_op jit(solution)/shard_map/ppermute | solution.py:218
  40.9 13.0 %collective-permute-start.20 = (f32[640,128]{1,0:T(8,128)S(1)}, f32[640,128]{1,0:T(8,128)S(1)}, u32[]{:S(2)}, u32[]{:S(2)}) collective-permute-start(f32[640,128]{1,0:T(8,128)S(1)} %constant_dynamic-slice_fusion.1), channel_id=1, source_target_pairs={{0,2},{1,3},{2,0},{3,1},{4,6},{5,7},{6,4},{7,5},{8,10},{9,11},{10,... | collective-permute-start | bytes 983048 | tf_op jit(solution)/shard_map/ppermute | solution.py:218
  49.4 5.6 %collective-permute-start.15 = (f32[2,512]{1,0:T(2,128)S(1)}, f32[2,512]{1,0:T(2,128)S(1)}, u32[]{:S(2)}, u32[]{:S(2)}) collective-permute-start(f32[2,512]{1,0:T(2,128)S(1)} %pad_maximum_fusion.2), channel_id=1, source_target_pairs={{0,6},{1,7},{2,4},{3,5},{4,2},{5,3},{6,0},{7,1},{8,14},{9,15},{10,... | collective-permute-start | bytes 12296 | tf_op jit(solution)/shard_map/ppermute | solution.py:218
  51.9 4.5 %collective-permute-start.14 = (f32[2,512]{1,0:T(2,128)S(1)}, f32[2,512]{1,0:T(2,128)S(1)}, u32[]{:S(2)}, u32[]{:S(2)}) collective-permute-start(f32[2,512]{1,0:T(2,128)S(1)} %pad_maximum_fusion.2), channel_id=1, source_target_pairs={{0,4},{1,5},{2,6},{3,7},{4,0},{5,1},{6,2},{7,3},{8,12},{9,13},{10,... | collective-permute-start | bytes 12296 | tf_op jit(solution)/shard_map/ppermute | solution.py:218
  51.9 4.5 %collective-permute-start.13 = (f32[2,512]{1,0:T(2,128)S(1)}, f32[2,512]{1,0:T(2,128)S(1)}, u32[]{:S(2)}, u32[]{:S(2)}) collective-permute-start(f32[2,512]{1,0:T(2,128)S(1)} %pad_maximum_fusion.2), channel_id=1, source_target_pairs={{0,2},{1,3},{2,0},{3,1},{4,6},{5,7},{6,4},{7,5},{8,10},{9,11},{10,... | collective-permute-start | bytes 12296 | tf_op jit(solution)/shard_map/ppermute | solution.py:218
  53.9 9.8 %collective-permute-start.21 = (f32[320,128]{1,0:T(8,128)S(1)}, f32[320,128]{1,0:T(8,128)S(1)}, u32[]{:S(2)}, u32[]{:S(2)}) collective-permute-start(f32[320,128]{1,0:T(8,128)S(1)} %constant_dynamic-slice_fusion), channel_id=1, source_target_pairs={{0,4},{1,5},{2,6},{3,7},{4,0},{5,1},{6,2},{7,3},{8,12},{9,13},{10,... | collective-permute-start | bytes 491528 | tf_op jit(solution)/shard_map/ppermute | solution.py:218
  56.5 7.2 %collective-permute-start.18 = (f32[8,512]{1,0:T(8,128)S(1)}, f32[8,512]{1,0:T(8,128)S(1)}, u32[]{:S(2)}, u32[]{:S(2)}) collective-permute-start(f32[8,512]{1,0:T(8,128)S(1)} %concatenate.22.refs_0_), channel_id=1, source_target_pairs={{0,24},{8,16},{16,8},{24,0},{1,25},{9,17},{17,9},{25,1},{2,26},{10... | collective-permute-start | bytes 49160 | tf_op jit(solution)/shard_map/ppermute | solution.py:218
  58.9 4.8 %collective-permute-start.17 = (f32[8,512]{1,0:T(8,128)S(1)}, f32[8,512]{1,0:T(8,128)S(1)}, u32[]{:S(2)}, u32[]{:S(2)}) collective-permute-start(f32[8,512]{1,0:T(8,128)S(1)} %concatenate.22.refs_0_), channel_id=1, source_target_pairs={{0,16},{8,24},{16,0},{24,8},{1,17},{9,25},{17,1},{25,9},{2,18},{10... | collective-permute-start | bytes 49160 | tf_op jit(solution)/shard_map/ppermute | solution.py:218
  59.4 4.3 %collective-permute-start.16 = (f32[8,512]{1,0:T(8,128)S(1)}, f32[8,512]{1,0:T(8,128)S(1)}, u32[]{:S(2)}, u32[]{:S(2)}) collective-permute-start(f32[8,512]{1,0:T(8,128)S(1)} %concatenate.22.refs_0_), channel_id=1, source_target_pairs={{0,8},{8,0},{16,24},{24,16},{1,9},{9,1},{17,25},{25,17},{2,10},{10... | collective-permute-start | bytes 49160 | tf_op jit(solution)/shard_map/ppermute | solution.py:218
  63.8 6.6 %collective-permute-start.23 = (f32[320,128]{1,0:T(8,128)S(1)}, f32[320,128]{1,0:T(8,128)S(1)}, u32[]{:S(2)}, u32[]{:S(2)}) collective-permute-start(f32[320,128]{1,0:T(8,128)S(1)} %dynamic-slice_add_fusion.1), channel_id=1, source_target_pairs={{0,2},{1,3},{2,0},{3,1},{4,6},{5,7},{6,4},{7,5},{8,10},{9,11},{10,... | collective-permute-start | bytes 491528 | tf_op jit(solution)/shard_map/ppermute | solution.py:218
  64.3 17.5 %collective-permute-start.25 = (f32[320,128]{1,0:T(8,128)S(1)}, f32[320,128]{1,0:T(8,128)S(1)}, u32[]{:S(2)}, u32[]{:S(2)}) collective-permute-start(f32[320,128]{1,0:T(8,128)S(1)} %dynamic-slice_add_fusion.1), channel_id=1, source_target_pairs={{0,6},{1,7},{2,4},{3,5},{4,2},{5,3},{6,0},{7,1},{8,14},{9,15},{10,... | collective-permute-start | bytes 491528 | tf_op jit(solution)/shard_map/ppermute | solution.py:218
  66.8 15.0 %collective-permute-start.24 = (f32[320,128]{1,0:T(8,128)S(1)}, f32[320,128]{1,0:T(8,128)S(1)}, u32[]{:S(2)}, u32[]{:S(2)}) collective-permute-start(f32[320,128]{1,0:T(8,128)S(1)} %dynamic-slice_add_fusion.1), channel_id=1, source_target_pairs={{0,4},{1,5},{2,6},{3,7},{4,0},{5,1},{6,2},{7,3},{8,12},{9,13},{10,... | collective-permute-start | bytes 491528 | tf_op jit(solution)/shard_map/ppermute | solution.py:218
  81.8 19.3 %collective-permute-start.26 = (f32[1280,128]{1,0:T(8,128)S(1)}, f32[1280,128]{1,0:T(8,128)S(1)}, u32[]{:S(2)}, u32[]{:S(2)}) collective-permute-start(f32[1280,128]{1,0:T(8,128)S(1)} %constant_dynamic-update-slice_fusion.refs_0_), channel_id=1, source_target_pairs={{0,1},{1,0},{2,3},{3,2},{4,5},{5,4},{6,7},{7,6},{8,9},{9,8},{10,11... | collective-permute-start | bytes 1966088 | tf_op jit(solution)/shard_map/ppermute | solution.py:218
  100.7 4.7 %collective-permute-start.22 = (f32[10,128,128]{2,1,0:T(8,128)}, f32[10,128,128]{2,1,0:T(8,128)S(1)}, u32[]{:S(2)}, u32[]{:S(2)}) collective-permute-start(f32[10,128,128]{2,1,0:T(8,128)} %covariance.2.mine_any), channel_id=1, source_target_pairs={{0,1},{1,0},{2,3},{3,2},{4,5},{5,4},{6,7},{7,6},{8,9},{9,8},{10,11... | collective-permute-start | bytes 1966088 | tf_op jit(solution)/shard_map/ppermute | solution.py:218
  136.2 5.5 %collective-permute-start.3 = (f32[2,512]{1,0:T(2,128)S(1)}, f32[2,512]{1,0:T(2,128)S(1)}, u32[]{:S(2)}, u32[]{:S(2)}) collective-permute-start(f32[2,512]{1,0:T(2,128)S(1)} %pad_maximum_fusion.4), channel_id=1, source_target_pairs={{0,6},{1,7},{2,4},{3,5},{4,2},{5,3},{6,0},{7,1},{8,14},{9,15},{10,... | collective-permute-start | bytes 12296 | tf_op jit(solution)/shard_map/while/body/eval_jaxpr/ppermute | solution.py:218
  138.7 4.5 %collective-permute-start.2 = (f32[2,512]{1,0:T(2,128)S(1)}, f32[2,512]{1,0:T(2,128)S(1)}, u32[]{:S(2)}, u32[]{:S(2)}) collective-permute-start(f32[2,512]{1,0:T(2,128)S(1)} %pad_maximum_fusion.4), channel_id=1, source_target_pairs={{0,4},{1,5},{2,6},{3,7},{4,0},{5,1},{6,2},{7,3},{8,12},{9,13},{10,... | collective-permute-start | bytes 12296 | tf_op jit(solution)/shard_map/while/body/eval_jaxpr/ppermute | solution.py:218
  138.7 4.5 %collective-permute-start.1 = (f32[2,512]{1,0:T(2,128)S(1)}, f32[2,512]{1,0:T(2,128)S(1)}, u32[]{:S(2)}, u32[]{:S(2)}) collective-permute-start(f32[2,512]{1,0:T(2,128)S(1)} %pad_maximum_fusion.4), channel_id=1, source_target_pairs={{0,2},{1,3},{2,0},{3,1},{4,6},{5,7},{6,4},{7,5},{8,10},{9,11},{10,... | collective-permute-start | bytes 12296 | tf_op jit(solution)/shard_map/while/body/eval_jaxpr/ppermute | solution.py:218
  143.2 4.8 %collective-permute-start.6 = (f32[8,512]{1,0:T(8,128)S(1)}, f32[8,512]{1,0:T(8,128)S(1)}, u32[]{:S(2)}, u32[]{:S(2)}) collective-permute-start(f32[8,512]{1,0:T(8,128)S(1)} %concatenate.25.refs_0_), channel_id=1, source_target_pairs={{0,24},{8,16},{16,8},{24,0},{1,25},{9,17},{17,9},{25,1},{2,26},{10... | collective-permute-start | bytes 49160 | tf_op jit(solution)/shard_map/while/body/eval_jaxpr/ppermute | solution.py:218
  145.6 3.7 %collective-permute-start.5 = (f32[8,512]{1,0:T(8,128)S(1)}, f32[8,512]{1,0:T(8,128)S(1)}, u32[]{:S(2)}, u32[]{:S(2)}) collective-permute-start(f32[8,512]{1,0:T(8,128)S(1)} %concatenate.25.refs_0_), channel_id=1, source_target_pairs={{0,16},{8,24},{16,0},{24,8},{1,17},{9,25},{17,1},{25,9},{2,18},{10... | collective-permute-start | bytes 49160 | tf_op jit(solution)/shard_map/while/body/eval_jaxpr/ppermute | solution.py:218
  146.2 3.7 %collective-permute-start.4 = (f32[8,512]{1,0:T(8,128)S(1)}, f32[8,512]{1,0:T(8,128)S(1)}, u32[]{:S(2)}, u32[]{:S(2)}) collective-permute-start(f32[8,512]{1,0:T(8,128)S(1)} %concatenate.25.refs_0_), channel_id=1, source_target_pairs={{0,8},{8,0},{16,24},{24,16},{1,9},{9,1},{17,25},{25,17},{2,10},{10... | collective-permute-start | bytes 49160 | tf_op jit(solution)/shard_map/while/body/eval_jaxpr/ppermute | solution.py:218
  169.2 2.3 collective-permute-start.7
  202.0 5.5 %collective-permute-start.3 = (f32[2,512]{1,0:T(2,128)S(1)}, f32[2,512]{1,0:T(2,128)S(1)}, u32[]{:S(2)}, u32[]{:S(2)}) collective-permute-start(f32[2,512]{1,0:T(2,128)S(1)} %pad_maximum_fusion.4), channel_id=1, source_target_pairs={{0,6},{1,7},{2,4},{3,5},{4,2},{5,3},{6,0},{7,1},{8,14},{9,15},{10,... | collective-permute-start | bytes 12296 | tf_op jit(solution)/shard_map/while/body/eval_jaxpr/ppermute | solution.py:218
  203.6 4.5 %collective-permute-start.2 = (f32[2,512]{1,0:T(2,128)S(1)}, f32[2,512]{1,0:T(2,128)S(1)}, u32[]{:S(2)}, u32[]{:S(2)}) collective-permute-start(f32[2,512]{1,0:T(2,128)S(1)} %pad_maximum_fusion.4), channel_id=1, source_target_pairs={{0,4},{1,5},{2,6},{3,7},{4,0},{5,1},{6,2},{7,3},{8,12},{9,13},{10,... | collective-permute-start | bytes 12296 | tf_op jit(solution)/shard_map/while/body/eval_jaxpr/ppermute | solution.py:218
  204.6 3.6 %collective-permute-start.1 = (f32[2,512]{1,0:T(2,128)S(1)}, f32[2,512]{1,0:T(2,128)S(1)}, u32[]{:S(2)}, u32[]{:S(2)}) collective-permute-start(f32[2,512]{1,0:T(2,128)S(1)} %pad_maximum_fusion.4), channel_id=1, source_target_pairs={{0,2},{1,3},{2,0},{3,1},{4,6},{5,7},{6,4},{7,5},{8,10},{9,11},{10,... | collective-permute-start | bytes 12296 | tf_op jit(solution)/shard_map/while/body/eval_jaxpr/ppermute | solution.py:218
  208.3 4.7 %collective-permute-start.6 = (f32[8,512]{1,0:T(8,128)S(1)}, f32[8,512]{1,0:T(8,128)S(1)}, u32[]{:S(2)}, u32[]{:S(2)}) collective-permute-start(f32[8,512]{1,0:T(8,128)S(1)} %concatenate.25.refs_0_), channel_id=1, source_target_pairs={{0,24},{8,16},{16,8},{24,0},{1,25},{9,17},{17,9},{25,1},{2,26},{10... | collective-permute-start | bytes 49160 | tf_op jit(solution)/shard_map/while/body/eval_jaxpr/ppermute | solution.py:218
  209.9 3.7 %collective-permute-start.5 = (f32[8,512]{1,0:T(8,128)S(1)}, f32[8,512]{1,0:T(8,128)S(1)}, u32[]{:S(2)}, u32[]{:S(2)}) collective-permute-start(f32[8,512]{1,0:T(8,128)S(1)} %concatenate.25.refs_0_), channel_id=1, source_target_pairs={{0,16},{8,24},{16,0},{24,8},{1,17},{9,25},{17,1},{25,9},{2,18},{10... | collective-permute-start | bytes 49160 | tf_op jit(solution)/shard_map/while/body/eval_jaxpr/ppermute | solution.py:218
  210.4 3.7 %collective-permute-start.4 = (f32[8,512]{1,0:T(8,128)S(1)}, f32[8,512]{1,0:T(8,128)S(1)}, u32[]{:S(2)}, u32[]{:S(2)}) collective-permute-start(f32[8,512]{1,0:T(8,128)S(1)} %concatenate.25.refs_0_), channel_id=1, source_target_pairs={{0,8},{8,0},{16,24},{24,16},{1,9},{9,1},{17,25},{25,17},{2,10},{10... | collective-permute-start | bytes 49160 | tf_op jit(solution)/shard_map/while/body/eval_jaxpr/ppermute | solution.py:218
  (25 other events, 189.9 us)
